TPU v7x, 32 devices: a whole 2x2x4 slice. The times are simulated.
32 devices in a mesh: dp: 4 (over y, x), fsdp: 8 (over z, core).
Axes of the slice: x: 2, y: 2, z: 4, core: 2. Of those that a mesh axis runs over, the one named last changes fastest.
Arguments:
- hidden: bfloat16 [16384, 1536], P(('dp', 'fsdp')), may hold values from -6 to 6
- lengths: int32 [512], P(('dp', 'fsdp')), may hold values from 1 to 32
- norm_gain: float32 [1536], replicated, may hold values from 0.1 to 1.9
- up_weight: bfloat16 [1536, 3072], P('fsdp'), may hold values from -0.15625 to 0.15625
- down_weight: bfloat16 [3072, 1536], P('fsdp'), may hold values from -0.109375 to 0.109375
- pool_gain: float32 [1536], replicated, may hold values from 0.1 to 1.9
- proj_weight: bfloat16 [1536, 768], P('fsdp'), may hold values from -1 to 1
- owners: int32 [512, 1], P(('dp', 'fsdp')), may hold values from 0 to 3; in each aligned block of 16 rows (0 to 15, 16 to 31, ...) at most 8 rows name the same one
Outputs:
- owned: bfloat16 [1024, 768], P(('dp', 'fsdp'))
Inputs may be any that keep to these rules, and one draw needn't show every extreme that they name: `owners`: in each aligned block of 16 passages no owner is named by more than 8 passages, a bound that some block reaches.
All inputs are finite; a program needn't handle non-finite values.
Results may differ from a plain program's by a relative error of at most 0.014.
Values may be sent and summed in bfloat16 or wider, within the bound.
A program may use at most 128 MiB of HBM per device.

v0:
```python
import jax
import jax.numpy as jnp
from jax import lax
from jax.sharding import PartitionSpec as P

ITERS = 4


RIDGE_TERM = 1.0
EPSILON = 1e-06
PRECISE = lax.Precision.HIGHEST


def rms_scale(values, gain_vector):
    return (
        values
        * lax.rsqrt(jnp.mean(values * values, axis=-1, keepdims=True) + EPSILON)
        * gain_vector
    )


def build_covariance(full_sums, average_sum, row_count):
    average = average_sum / row_count
    eye_matrix = jnp.eye(full_sums.shape[0], dtype=jnp.float32)
    covariance = (
        full_sums / row_count - average[:, None] * average[None, :] + RIDGE_TERM * eye_matrix
    )
    magnitude = jnp.sqrt(jnp.sum(covariance * covariance))
    initial = 4.0 / magnitude * eye_matrix - 4.0 * covariance / (magnitude * magnitude)
    return (covariance, average, initial)


def newton_update(iterate_rows, covariance, iterate_full):
    mixed = jnp.dot(
        jnp.dot(iterate_rows, covariance, precision=PRECISE, preferred_element_type=jnp.float32),
        iterate_full,
        precision=PRECISE,
        preferred_element_type=jnp.float32,
    )
    return 2.0 * iterate_rows - mixed


def last_update_rows(centered, covariance, iterate_full):
    row_product = jnp.dot(
        centered, iterate_full, precision=PRECISE, preferred_element_type=jnp.float32
    )
    row_mixed = jnp.dot(
        jnp.dot(row_product, covariance, precision=PRECISE, preferred_element_type=jnp.float32),
        iterate_full,
        precision=PRECISE,
        preferred_element_type=jnp.float32,
    )
    return 2.0 * row_product - row_mixed


def on_device(hidden, lengths, norm_gain, up_weight, down_weight, pool_gain, proj_weight, owners):
    tok_rows = hidden.shape[0]
    pass_rows = lengths.shape[0]
    seq_len = tok_rows // pass_rows
    normed = rms_scale(hidden.astype(jnp.float32), norm_gain).astype(jnp.bfloat16)
    columns = normed
    hidden_pre = jnp.dot(
        columns,
        lax.all_gather(up_weight, "fsdp", axis=0, tiled=True),
        preferred_element_type=jnp.float32,
    )
    activated = jax.nn.gelu(hidden_pre, approximate=True).astype(jnp.bfloat16)
    columns = activated
    branch = jnp.dot(
        columns,
        lax.all_gather(down_weight, "fsdp", axis=0, tiled=True),
        preferred_element_type=jnp.float32,
    )
    layer_out = (hidden.astype(jnp.float32) + branch).astype(jnp.bfloat16)
    token_index = lax.broadcasted_iota(jnp.int32, (pass_rows, tok_rows), 1)
    passage_index = lax.broadcasted_iota(jnp.int32, (pass_rows, tok_rows), 0)
    inside = (token_index // seq_len == passage_index) & (token_index % seq_len < lengths[:, None])
    pooled = (
        jnp.dot(inside.astype(jnp.bfloat16), layer_out, preferred_element_type=jnp.float32)
        / lengths.astype(jnp.float32)[:, None]
    )
    pool_normed = rms_scale(pooled, pool_gain).astype(jnp.bfloat16)
    columns = pool_normed
    embedded = jnp.dot(
        columns,
        lax.all_gather(proj_weight, "fsdp", axis=0, tiled=True),
        preferred_element_type=jnp.float32,
    )
    products = jnp.dot(embedded.T, embedded, precision=PRECISE, preferred_element_type=jnp.float32)
    column_sum = jnp.sum(embedded, axis=0)
    total_rows = float(pass_rows * lax.axis_size("dp") * lax.axis_size("fsdp"))
    full_sums, average_sum = lax.psum((products, column_sum), ("dp", "fsdp"))
    covariance, average, iterate_full = build_covariance(full_sums, average_sum, total_rows)
    for iteration in range(ITERS - 2):
        iterate_full = newton_update(iterate_full, covariance, iterate_full)
    whitened = last_update_rows(embedded - average, covariance, iterate_full).astype(jnp.bfloat16)
    owner_count = lax.axis_size("dp")
    capacity = 2 * pass_rows // owner_count
    target_owner = owners[:, 0]
    position = lax.broadcasted_iota(jnp.int32, (pass_rows, pass_rows), 0)
    previous = lax.broadcasted_iota(jnp.int32, (pass_rows, pass_rows), 1)
    earlier = (target_owner[:, None] == target_owner[None, :]) & (previous < position)
    target = target_owner * capacity + jnp.sum(earlier.astype(jnp.int32), axis=1)
    slot_index = lax.broadcasted_iota(jnp.int32, (owner_count * capacity, pass_rows), 0)
    selector = (slot_index == target[None, :]).astype(jnp.bfloat16)
    outgoing = jnp.dot(selector, whitened, preferred_element_type=jnp.float32).astype(jnp.bfloat16)
    return lax.all_to_all(outgoing, "dp", split_axis=0, concat_axis=0, tiled=True)


def solution(mesh):
    placed = (
        P(("dp", "fsdp"), None),
        P(("dp", "fsdp")),
        P(),
        P("fsdp", None),
        P("fsdp", None),
        P(),
        P("fsdp", None),
        P(("dp", "fsdp"), None),
    )
    return jax.shard_map(
        on_device, mesh=mesh, in_specs=placed, out_specs=P(("dp", "fsdp"), None), check_vma=False
    )
```

profile of v0, /device:TPU:0, one launch (start us, length us, event | category | flops | bytes accessed | tf_op | source)
XLA Modules:
  0.0 415.6 jit_solution(10799612231338822403)
XLA Ops:
  6.5 0.7 all-gather.4.cloned.1.call-update
  7.3 0.7 all-gather.6.cloned.1.call-update
  8.1 0.7 all-gather.8.cloned.1.call-update
  8.9 0.4 fusion.8
  9.3 93.2 %all-gather.4.cloned.1.call-done = bf16[1536,3072]{1,0:T(8,128)(2,1)} async-done(((bf16[192,3072]{1,0:T(8,128)(2,1)}), bf16[1536,3072]{1,0:T(8,128)(2,1)}) %all-gather.4.cloned.1.call-update) | async-done | bytes 9437200 | tf_op jit(solution)/shard_map/all_gather | solution.py:64
  102.5 90.9 %all-gather.6.cloned.1.call-done = bf16[3072,1536]{1,0:T(8,128)(2,1)} async-done(((bf16[384,1536]{1,0:T(8,128)(2,1)}), bf16[3072,1536]{1,0:T(8,128)(2,1)}) %all-gather.6.cloned.1.call-update) | async-done | bytes 9437200 | tf_op jit(solution)/shard_map/all_gather | solution.py:71
  193.3 16.5 %fusion.16 = bf16[512,1536]{1,0:T(8,128)(2,1)S(1)} fusion(bf16[3072,1536]{1,0:T(8,128)(2,1)} %all-gather.6.cloned.1.call-done, bf16[512,1536]{1,0:T(8,128)(2,1)S(1)} %copy-done.1, bf16[1536,3072]{1,0:T(8,128)(2,1)} %all-gather.4.cloned.1.call-done, f32[1536]{0:T(1024)S(1)} %copy-done.4, f32[512]{0:T(512)S(1)} %add_rsqrt_fusion), kind=kOutput, calls=%fused_computation.19 | convolution fusion | flops 9683337216 | bytes 22028288 | tf_op jit(solution)/shard_map/dot_general | solution.py:69
  209.8 0.5 multiply_reduce_fusion.1
  210.3 14.8 %all-gather.8.cloned.1.call-done = bf16[1536,768]{1,0:T(8,128)(2,1)} async-done(((bf16[192,768]{1,0:T(8,128)(2,1)}), bf16[1536,768]{1,0:T(8,128)(2,1)}) %all-gather.8.cloned.1.call-update) | async-done | bytes 2359312 | tf_op jit(solution)/shard_map/all_gather | solution.py:86
  225.1 2.1 fusion.73
  227.2 3.5 fusion.74
  230.7 0.2 convert_reduce_fusion
  230.9 40.1 %psum.14 = f32[768]{0:T(1024)S(1)} all-reduce(f32[768]{0:T(1024)S(1)} %get-tuple-element.7), channel_id=1, replica_groups=mesh['dp'=4,'fsdp'=8] {'dp','fsdp'}, use_global_device_ids=true, to_apply=%region_4.5 | all-reduce | flops 768 | bytes 6144 | tf_op jit(solution)/shard_map/psum | solution.py:92
  271.1 94.2 %all-reduce.2.cloned.1.call-done = f32[768,768]{1,0:T(8,128)} async-done(((f32[768,768]{1,0:T(8,128)}), f32[768,768]{1,0:T(8,128)}) %all-reduce.2.cloned.1.call-update) | async-done | bytes 2359312 | tf_op jit(solution)/shard_map/psum | solution.py:92
  365.3 3.2 multiply_reduce_fusion
  369.3 6.7 %fusion.19 = f32[768,768]{1,0:T(8,128)S(1)} fusion(f32[]{:T(128)S(6)} %mul.135, f32[]{:T(128)S(6)} %div.58, f32[768,768]{1,0:T(8,128)S(1)} %copy-done, f32[768]{0:T(1024)S(1)} %broadcast_multiply_fusion), kind=kOutput, calls=%fused_computation.27 | convolution fusion | flops 5445255168 | bytes 4721672 | tf_op jit(solution)/shard_map/dot_general | solution.py:35
  376.0 6.9 %multiply_subtract_fusion.1 = f32[768,768]{1,0:T(8,128)S(1)} fusion(f32[768,768]{1,0:T(8,128)S(1)} %fusion.19, f32[]{:T(128)S(6)} %mul.135, f32[]{:T(128)S(6)} %div.58, f32[768]{0:T(1024)S(1)} %broadcast_multiply_fusion, f32[768,768]{1,0:T(8,128)S(1)} %copy-done), kind=kOutput, calls=%fused_computation.21 | convolution fusion | flops 5448794112 | bytes 7080968 | tf_op jit(solution)/shard_map/dot_general | solution.py:34
  383.0 6.4 %fusion.72 = f32[768,768]{1,0:T(8,128)S(1)} fusion(f32[768,768]{1,0:T(8,128)S(1)} %multiply_subtract_fusion.1, f32[768,768]{1,0:T(8,128)S(1)} %copy-done, f32[768]{0:T(1024)S(1)} %broadcast_multiply_fusion), kind=kOutput, calls=%fused_computation.89 | convolution fusion | flops 5439356928 | bytes 7080960 | tf_op jit(solution)/shard_map/dot_general | solution.py:35
  389.3 6.1 %multiply_subtract_fusion = f32[768,768]{1,0:T(8,128)S(1)} fusion(f32[768,768]{1,0:T(8,128)S(1)} %multiply_subtract_fusion.1, f32[768,768]{1,0:T(8,128)S(1)} %fusion.72), kind=kOutput, calls=%fused_computation.20 | convolution fusion | flops 5436997632 | bytes 7077888 | tf_op jit(solution)/shard_map/dot_general | solution.py:34
  395.4 1.5 fusion.41
  396.9 1.6 fusion.71
  398.5 1.3 fusion.39
  399.9 8.1 %all_to_all.12 = bf16[4,8,768]{2,1,0:T(8,128)(2,1)S(1)} all-to-all(bf16[4,8,768]{2,1,0:T(8,128)(2,1)S(1)} %fusion.38), channel_id=1, replica_groups=mesh['dp'=4,'fsdp'=8] {'dp'}, dimensions={0} | all-to-all | bytes 98304 | tf_op jit(solution)/shard_map/all_to_all | solution.py:107
  408.0 0.6 copy.11
  (26 shorter events, 0.3 us)
Async XLA Ops:
  6.5 2.3 copy-start.3
  6.5 2.3 copy-start.1
  6.5 186.8 %copy-start.4 = (f32[1536]{0:T(1024)S(1)}, f32[1536]{0:T(1024)}, u32[]{:S(2)}) copy-start(f32[1536]{0:T(1024)} %param.10) | copy-start | bytes 18436
  6.5 95.9 %all-gather.4.cloned.1.call-start = ((), (), s32[]{:S(2)}) async-start(), calls=%async_computation.1 | async-start | bytes 10616832 | tf_op jit(solution)/shard_map/all_gather | solution.py:64
  7.3 186.1 %all-gather.6.cloned.1.call-start = ((), (), s32[]{:S(2)}) async-start(), calls=%async_computation.2 | async-start | bytes 10616832 | tf_op jit(solution)/shard_map/all_gather | solution.py:71
  8.0 217.1 %all-gather.8.cloned.1.call-start = ((), (), s32[]{:S(2)}) async-start(), calls=%async_computation.3 | async-start | bytes 2654208 | tf_op jit(solution)/shard_map/all_gather | solution.py:86
  8.7 356.5 %all-reduce.2.cloned.1.call-start = ((), (), s32[]{:S(2)}) async-start(), calls=%async_computation.4 | async-start | bytes 4718592 | tf_op jit(solution)/shard_map/psum | solution.py:92
  9.3 215.8 %copy-start.2 = (f32[1536]{0:T(1024)S(1)}, f32[1536]{0:T(1024)}, u32[]{:S(2)}) copy-start(f32[1536]{0:T(1024)} %param.13) | copy-start | bytes 18436
  227.2 3.5 copy-start.5
  365.3 4.0 copy-start
Sparse Core Ops, SparseCore 0:
  9.0 93.4 all-gather.3
  104.1 89.1 all-gather.5
  195.0 30.0 all-gather.7
  230.8 134.3 all-reduce.1
where the time goes:
time: 424 us; the launch traced here: 416 us
  waiting for transfers between devices  295 us (70%)
  matrix products  53.1 us (13%)
  blocking collectives  48.3 us (11%)
  between operations  14.5 us (3%)
    psum x1, waiting for transfers between devices, on_device(): full_sums, average_sum = lax.psum((products, column_sum), ('dp', 'fsdp'))  94.2 us
    all_gather x1, waiting for transfers between devices, on_device(): lax.all_gather(up_weight, 'fsdp', axis=0, tiled=True)  93.2 us
    all_gather x1, waiting for transfers between devices, on_device(): lax.all_gather(down_weight, 'fsdp', axis=0, tiled=True)  90.9 us
    psum x1, blocking collectives, on_device(): full_sums, average_sum = lax.psum((products, column_sum), ('dp', 'fsdp'))  40.1 us
    dot_general x1, matrix products, on_device(): jnp.dot(columns, lax.all_gather(down_weight, 'fsdp', axis=0, tiled=True),...  16.5 us
    all_gather x1, waiting for transfers between devices, on_device(): lax.all_gather(proj_weight, 'fsdp', axis=0, tiled=True)  14.8 us
    dot_general x2, matrix products, newton_update(): jnp.dot(iterate_rows, covariance, precision=PRECISE, preferred_element_ty...  13.1 us
    dot_general x2, matrix products, newton_update(): jnp.dot(jnp.dot(iterate_rows, covariance, precision=PRECISE, preferred_el...  13 us
  transfers between devices with their start and end apart: 4, of which 4 were waited for; matrix products, arithmetic and copies ran while one was open for 4% of the time, Pallas kernels for 0%

commit v1 on v0

v1 whole, which is shorter than its diff:
```python
import jax
import jax.numpy as jnp
from jax import lax
from jax.sharding import PartitionSpec as P

RIDGE_TERM = 1.0
EPSILON = 1e-06
HIGH = lax.Precision.HIGH


def fdot(a, b):
    return jnp.dot(a, b, precision=HIGH, preferred_element_type=jnp.float32)


def exchange(blocks):
    return lax.all_to_all(blocks, "fsdp", split_axis=0, concat_axis=0, tiled=True)


def on_device(hidden, lengths, norm_gain, up_weight, down_weight, pool_gain, proj_weight, owners):
    tok_rows, width = hidden.shape
    pass_rows = lengths.shape[0]
    seq_len = tok_rows // pass_rows
    n_fsdp = lax.axis_size("fsdp")
    n_dp = lax.axis_size("dp")
    me = lax.axis_index("fsdp")
    ff_rows = down_weight.shape[0]
    d_rows, emb = proj_weight.shape
    group = n_fsdp * pass_rows
    hidden32 = hidden.astype(jnp.float32)
    normed = (
        hidden32
        * lax.rsqrt(jnp.mean(hidden32 * hidden32, axis=-1, keepdims=True) + EPSILON)
        * norm_gain
    ).astype(jnp.bfloat16)
    hidden_pre = jnp.dot(
        normed,
        lax.all_gather(up_weight, "fsdp", axis=0, tiled=True),
        preferred_element_type=jnp.float32,
    )
    activated = jax.nn.gelu(hidden_pre, approximate=True).astype(jnp.bfloat16)
    token_index = lax.broadcasted_iota(jnp.int32, (pass_rows, tok_rows), 1)
    passage_index = lax.broadcasted_iota(jnp.int32, (pass_rows, tok_rows), 0)
    inside = (
        (token_index // seq_len == passage_index) & (token_index % seq_len < lengths[:, None])
    ).astype(jnp.bfloat16)
    inverse = 1.0 / lengths.astype(jnp.float32)[:, None]
    act_mean = jnp.dot(inside, activated, preferred_element_type=jnp.float32) * inverse
    hid_mean = jnp.dot(inside, hidden, preferred_element_type=jnp.float32) * inverse
    packed = jnp.concatenate(
        [
            act_mean.reshape(pass_rows, n_fsdp, ff_rows),
            hid_mean.reshape(pass_rows, n_fsdp, d_rows),
        ],
        axis=2,
    ).transpose(1, 0, 2)
    pooled_in = exchange(packed).reshape(group, ff_rows + d_rows)
    partial = fdot(pooled_in[:, :ff_rows], down_weight.astype(jnp.float32))
    partial = partial.reshape(group, n_fsdp, d_rows).transpose(1, 0, 2)
    pooled = jnp.sum(exchange(partial), axis=0) + pooled_in[:, ff_rows:]
    squares = jnp.sum(pooled * pooled, axis=1, keepdims=True)
    gain = lax.dynamic_slice(pool_gain, (me * d_rows,), (d_rows,))
    emb_part = fdot(pooled * gain, proj_weight.astype(jnp.float32))
    emb_part = jnp.concatenate([emb_part, jnp.broadcast_to(squares, (group, 128))], axis=1)
    summed = jnp.sum(exchange(emb_part.reshape(n_fsdp, pass_rows, emb + 128)), axis=0)
    embedded = summed[:, :emb] * lax.rsqrt(summed[:, emb : emb + 1] / width + EPSILON)
    everyone = lax.all_gather(embedded, ("dp", "fsdp"), axis=0, tiled=True)
    total_rows = float(everyone.shape[0])
    average = jnp.sum(everyone, axis=0) / total_rows
    eye = jnp.eye(emb, dtype=jnp.float32)
    covariance = (
        fdot(everyone.T, everyone) / total_rows
        - average[:, None] * average[None, :]
        + RIDGE_TERM * eye
    )
    magnitude = jnp.sqrt(jnp.sum(covariance * covariance))
    s1 = eye - (2.0 / magnitude) * covariance
    s2 = fdot(s1, s1)
    s4 = fdot(s2, s2)
    rows = (embedded - average) * (2.0 / magnitude)
    rows = rows + fdot(rows, s1)
    rows = rows + fdot(rows, s2)
    rows = rows + fdot(rows, s4)
    rows = rows + fdot(fdot(rows, s4), s4)
    whitened = rows.astype(jnp.bfloat16)
    capacity = 2 * pass_rows // n_dp
    target_owner = owners[:, 0]
    position = lax.broadcasted_iota(jnp.int32, (pass_rows, pass_rows), 0)
    previous = lax.broadcasted_iota(jnp.int32, (pass_rows, pass_rows), 1)
    earlier = (target_owner[:, None] == target_owner[None, :]) & (previous < position)
    target = target_owner * capacity + jnp.sum(earlier.astype(jnp.int32), axis=1)
    slot_index = lax.broadcasted_iota(jnp.int32, (n_dp * capacity, pass_rows), 0)
    selector = (slot_index == target[None, :]).astype(jnp.bfloat16)
    outgoing = jnp.dot(selector, whitened, preferred_element_type=jnp.float32).astype(jnp.bfloat16)
    return lax.all_to_all(outgoing, "dp", split_axis=0, concat_axis=0, tiled=True)


def solution(mesh):
    placed = (
        P(("dp", "fsdp"), None),
        P(("dp", "fsdp")),
        P(),
        P("fsdp", None),
        P("fsdp", None),
        P(),
        P("fsdp", None),
        P(("dp", "fsdp"), None),
    )
    return jax.shard_map(
        on_device, mesh=mesh, in_specs=placed, out_specs=P(("dp", "fsdp"), None), check_vma=False
    )
```

time: 424 us -> 256 us (0.60); the launches traced: 416 us -> 256 us
  waiting for transfers between devices: 295 us -> 167 us
  matrix products: 53.1 us -> 28.1 us
  blocking collectives: 48.3 us -> 37.2 us
    psum x1 -> x0, waiting for transfers between devices: 94.2 us -> none  [on_device(): full_sums, average_sum = lax.psum((products, column_sum), ('dp', 'fsdp'))]
    all_gather x2 -> x1, waiting for transfers between devices: 106 us -> 53.9 us  [on_device(): everyone = lax.all_gather(embedded, ('dp', 'fsdp'), axis=0, tiled=True)]
    psum x1 -> x0, blocking collectives: 40.1 us -> none  [on_device(): full_sums, average_sum = lax.psum((products, column_sum), ('dp', 'fsdp'))]
    all_to_all x0 -> x2, blocking collectives: none -> 29.9 us  [exchange(): lax.all_to_all(blocks, 'fsdp', split_axis=0, concat_axis=0, tiled=True)]
    dot_general x11 -> x12, matrix products: 53 us -> 28 us  [the longest x10 17.6 us: fdot(): return jnp.dot(a, b, precision=HIGH, preferred_element_type=jnp.float32)]
    all_to_all x0 -> x1, waiting for transfers between devices: none -> 19.9 us  [exchange(): lax.all_to_all(blocks, 'fsdp', split_axis=0, concat_axis=0, tiled=True)]
  transfers between devices with their start and end apart: 4 -> 3, of which waited for: 4 -> 3; matrix products, arithmetic and copies ran while one was open for 4% -> 2% of each run, Pallas kernels for 0% -> 0%
where the time goes in v1:
time: 256 us
  waiting for transfers between devices  167 us (65%)
  blocking collectives  37.2 us (15%)
  matrix products  28.1 us (11%)
  between operations  14.2 us (6%)
  other arithmetic  3.84 us (2%)
  starting transfers between devices  3.62 us (1%)
    all_gather x1, waiting for transfers between devices, on_device(): lax.all_gather(up_weight, 'fsdp', axis=0, tiled=True)  92.1 us
    all_gather x1, waiting for transfers between devices, on_device(): everyone = lax.all_gather(embedded, ('dp', 'fsdp'), axis=0, tiled=True)  53.9 us
    all_to_all x2, blocking collectives, exchange(): lax.all_to_all(blocks, 'fsdp', split_axis=0, concat_axis=0, tiled=True)  29.9 us
    all_to_all x1, waiting for transfers between devices, exchange(): lax.all_to_all(blocks, 'fsdp', split_axis=0, concat_axis=0, tiled=True)  19.9 us
    dot_general x10, matrix products, fdot(): return jnp.dot(a, b, precision=HIGH, preferred_element_type=jnp.float32)  17.6 us
    dot_general x1, matrix products, on_device(): jnp.dot(inside, activated, preferred_element_type=jnp.float32) * inverse  8.59 us
    all_to_all x1, blocking collectives, on_device(): lax.all_to_all(outgoing, 'dp', split_axis=0, concat_axis=0, tiled=True)  7.33 us
  transfers between devices with their start and end apart: 3, of which 3 were waited for; matrix products, arithmetic and copies ran while one was open for 2% of the time, Pallas kernels for 0%

profile of v1, /device:TPU:0, one launch (start us, length us, event | category | flops | bytes accessed | tf_op | source)
XLA Modules:
  0.0 255.5 jit_solution(67305283520336253)
XLA Ops:
  6.6 0.7 all-gather.3.cloned.1.call-update
  7.3 0.7 convert_divide_fusion
  8.0 1.8 convolution_multiply_fusion.1
  10.3 92.1 %all-gather.3.cloned.1.call-done = bf16[1536,3072]{1,0:T(8,128)(2,1)} async-done(((bf16[192,3072]{1,0:T(8,128)(2,1)}), bf16[1536,3072]{1,0:T(8,128)(2,1)}) %all-gather.3.cloned.1.call-update) | async-done | bytes 9437200 | tf_op jit(solution)/shard_map/all_gather | solution.py:37
  102.5 8.6 %convolution_multiply_fusion = f32[16,3072]{1,0:T(8,128)S(1)} fusion(bf16[1536,3072]{1,0:T(8,128)(2,1)} %all-gather.3.cloned.1.call-done, bf16[512,1536]{1,0:T(8,128)(2,1)S(1)} %copy-done.1, f32[1536]{0:T(1024)S(1)} %copy-done.5, f32[512]{0:T(512)S(1)} %add_rsqrt_fusion, f32[16]{0:T(128)S(1)} %convert_divide_fusion, s32[16]{0:T(128)S(1)} %copy-done.4, ...), kind=kOutput, calls=%fused_computation.11 | convolution fusion | flops 4899561472 | bytes 11224192 | tf_op jit(solution)/shard_map/dot_general | solution.py:47
  111.1 13.5 %all_to_all.27 = f32[8,16,576]{2,1,0:T(8,128)S(1)} all-to-all(f32[8,16,576]{2,1,0:T(8,128)S(1)} %maximum_bitcast_fusion), channel_id=1, replica_groups=mesh['dp'=4,'fsdp'=8] {'fsdp'}, dimensions={0} | all-to-all | bytes 589824 | tf_op jit(solution)/shard_map/all_to_all | solution.py:16
  124.7 1.9 fusion.29
  126.6 3.5 %all-to-all-start.1 = ((f32[8,128,192]{1,2,0:T(8,128)}), f32[8,128,192]{1,2,0:T(8,128)S(1)}, u32[]{:S(2)}, u32[]{:S(2)}) async-start(f32[8,128,192]{1,2,0:T(8,128)} %bitcast.4), calls=%async_computation.1 | async-start | bytes 1572864 | tf_op jit(solution)/shard_map/all_to_all | solution.py:16
  130.2 0.8 dynamic_slice.3
  131.1 19.9 %all-to-all-done.1 = f32[8,128,192]{1,2,0:T(8,128)S(1)} async-done(((f32[8,128,192]{1,2,0:T(8,128)}), f32[8,128,192]{1,2,0:T(8,128)S(1)}, u32[]{:S(2)}, u32[]{:S(2)}) %all-to-all-start.1) | async-done | bytes 786464 | tf_op jit(solution)/shard_map/all_to_all | solution.py:16
  151.6 16.4 %all_to_all.28 = f32[8,16,896]{2,1,0:T(8,128)S(1)} all-to-all(f32[8,16,896]{2,1,0:T(8,128)S(1)} %bitcast.33), channel_id=1, replica_groups=mesh['dp'=4,'fsdp'=8] {'fsdp'}, dimensions={0} | all-to-all | bytes 917504 | tf_op jit(solution)/shard_map/all_to_all | solution.py:16
  168.1 0.7 slice_multiply_fusion
  169.0 53.9 %all-gather.5.cloned.1.call-done = f32[512,768]{1,0:T(8,128)} async-done(((f32[16,768]{1,0:T(8,128)}), f32[512,768]{1,0:T(8,128)}) %all-gather.5.cloned.1.call-update) | async-done | bytes 1572880 | tf_op jit(solution)/shard_map/all_gather | solution.py:66
  223.0 1.5 reduce_sum.68
  224.5 5.1 %multiply_reduce_fusion = (f32[]{:T(128)}, f32[768,768]{1,0:T(8,128)S(1)}) fusion(f32[768]{0:T(1024)S(1)} %broadcast_multiply_fusion, f32[512,768]{1,0:T(8,128)} %all-gather.5.cloned.1.call-done), kind=kOutput, calls=%fused_computation.17 | convolution fusion | flops 1816657920 | bytes 3935236 | tf_op jit(solution)/shard_map/dot_general | solution.py:12
  230.3 3.2 %fusion.12 = f32[768,768]{1,0:T(8,128)S(1)} fusion(f32[768,768]{1,0:T(8,128)S(1)} %get-tuple-element.6, f32[]{:T(128)S(6)} %div.48), kind=kOutput, calls=%fused_computation.20 | convolution fusion | flops 2720268288 | bytes 4718596 | tf_op jit(solution)/shard_map/dot_general | solution.py:12
  233.5 0.9 fusion.26
  234.3 3.1 %fusion.57 = f32[768,768]{1,0:T(8,128)S(1)} fusion(f32[768,768]{1,0:T(8,128)S(1)} %fusion.12), kind=kOutput, calls=%fused_computation.79 | convolution fusion | flops 2717908992 | bytes 4718592 | tf_op jit(solution)/shard_map/dot_general | solution.py:12
  237.5 0.8 convolution_add_fusion.1
  238.2 0.8 convolution_add_fusion
  239.0 0.8 fusion.58
  239.8 0.8 fusion.28
  240.7 7.3 %all_to_all.29 = bf16[4,8,768]{2,1,0:T(8,128)(2,1)S(1)} all-to-all(bf16[4,8,768]{2,1,0:T(8,128)(2,1)S(1)} %fusion.27), channel_id=1, replica_groups=mesh['dp'=4,'fsdp'=8] {'dp'}, dimensions={0} | all-to-all | bytes 98304 | tf_op jit(solution)/shard_map/all_to_all | solution.py:94
  248.0 0.6 copy.26
  (39 shorter events, 1.9 us)
Async XLA Ops:
  6.5 118.1 %copy-start = (bf16[384,1536]{1,0:T(8,128)(2,1)S(1)}, bf16[384,1536]{1,0:T(8,128)(2,1)}, u32[]{:S(2)}) copy-start(bf16[384,1536]{1,0:T(8,128)(2,1)} %param.12) | copy-start | bytes 3538948
  6.5 95.9 %copy-start.4 = (s32[16]{0:T(128)S(1)}, s32[16]{0:T(128)}, u32[]{:S(2)}) copy-start(s32[16]{0:T(128)} %param.9) | copy-start | bytes 196
  6.5 3.4 %copy-start.1 = (bf16[512,1536]{1,0:T(8,128)(2,1)S(1)}, bf16[512,1536]{1,0:T(8,128)(2,1)}, u32[]{:S(2)}) copy-start(bf16[512,1536]{1,0:T(8,128)(2,1)} %param.8) | copy-start | bytes 4718596
  6.5 95.9 %copy-start.5 = (f32[1536]{0:T(1024)S(1)}, f32[1536]{0:T(1024)}, u32[]{:S(2)}) copy-start(f32[1536]{0:T(1024)} %param.10) | copy-start | bytes 18436
  6.5 95.9 %all-gather.3.cloned.1.call-start = ((), (), s32[]{:S(2)}) async-start(), calls=%async_computation.4 | async-start | bytes 10616832 | tf_op jit(solution)/shard_map/all_gather | solution.py:37
  124.7 26.4 %copy-start.3 = (bf16[192,768]{1,0:T(8,128)(2,1)S(1)}, bf16[192,768]{1,0:T(8,128)(2,1)}, u32[]{:S(2)}) copy-start(bf16[192,768]{1,0:T(8,128)(2,1)} %param.14) | copy-start | bytes 884740
  126.6 24.4 %all-to-all-start.1 = ((f32[8,128,192]{1,2,0:T(8,128)}), f32[8,128,192]{1,2,0:T(8,128)S(1)}, u32[]{:S(2)}, u32[]{:S(2)}) async-start(f32[8,128,192]{1,2,0:T(8,128)} %bitcast.4), calls=%async_computation.1 | async-start | bytes 1572864 | tf_op jit(solution)/shard_map/all_to_all | solution.py:16
  130.1 92.9 %all-gather.5.cloned.1.call-start = ((), (), s32[]{:S(2)}) async-start(), calls=%async_computation.5 | async-start | bytes 1622016 | tf_op jit(solution)/shard_map/all_gather | solution.py:66
  130.9 37.9 %copy-start.6 = (s32[16,1]{0,1:T(1,128)S(1)}, s32[16,1]{0,1:T(1,128)}, u32[]{:S(2)}) copy-start(s32[16,1]{0,1:T(1,128)} %param.15) | copy-start | bytes 196
  230.2 3.2 %copy-start.2 = (f32[16,768]{1,0:T(8,128)S(1)}, f32[16,768]{1,0:T(8,128)}, u32[]{:S(2)}) copy-start(f32[16,768]{1,0:T(8,128)} %slice_multiply_fusion) | copy-start | bytes 147460
Sparse Core Ops, SparseCore 0:
  9.0 93.4 all-gather.2
  169.0 53.9 all-gather.4

commit v2 on v1

--- a/solution.py
+++ b/solution.py
@@ -1,6 +1,10 @@
+import functools
+
 import jax
 import jax.numpy as jnp
 from jax import lax
+from jax.experimental import pallas as pl
+from jax.experimental.pallas import tpu as pltpu
 from jax.sharding import PartitionSpec as P
 
 RIDGE_TERM = 1.0
@@ -12,8 +16,224 @@
     return jnp.dot(a, b, precision=HIGH, preferred_element_type=jnp.float32)
 
 
-def exchange(blocks):
-    return lax.all_to_all(blocks, "fsdp", split_axis=0, concat_axis=0, tiled=True)
+MESH = pl.DeviceIdType.MESH
+PLANE = 4
+
+
+def remote(src, dst, send, recv, device):
+    return pltpu.make_async_remote_copy(
+        src_ref=src, dst_ref=dst, send_sem=send, recv_sem=recv, device_id=device, device_id_type=MESH
+    )
+
+
+def meet(devices):
+    barrier = pltpu.get_barrier_semaphore()
+    for device in devices:
+        pl.semaphore_signal(barrier, inc=1, device_id=device, device_id_type=MESH)
+    pl.semaphore_wait(barrier, len(devices))
+
+
+def mate(q, e):
+    if e == 1:
+        return q + 1 - 2 * (q % 2)
+    if e == 2:
+        return q + 2 - 4 * (q // 2)
+    return 3 - q
+
+
+def gather_kernel(
+    nz, up_ref, full_ref, own_sem, z_send, z_recv, p_send, p_recv, x_send, x_recv, f_send, f_recv
+):
+    i = lax.axis_index("dp")
+    j = lax.axis_index("fsdp")
+    z = j // 2
+    c = j % 2
+    q = i % PLANE
+    base = i - q
+    rows = up_ref.shape[0]
+    cols = up_ref.shape[1] // PLANE
+
+    def row_at(level):
+        return pl.ds(pl.multiple_of((level * 2 + c) * rows, rows), rows)
+
+    def col_at(part):
+        return pl.ds(pl.multiple_of(part * cols, cols), cols)
+
+    partner = (i, z * 2 + 1 - c)
+    z_peers = [(i, ((z + d) % nz) * 2 + c) for d in range(1, nz)]
+    mates = [(base + mate(q, e), j) for e in range(1, PLANE)]
+    meet([partner] + z_peers + mates)
+    own = pltpu.make_async_copy(up_ref, full_ref.at[row_at(z), :], own_sem)
+    pending = []
+
+    def send(src, dst, ssem, rsem, device):
+        copy = remote(src, dst, ssem, rsem, device)
+        copy.start()
+        pending.append(copy)
+        return copy
+
+    z_copies = [
+        send(
+            up_ref.at[:, col_at(q)], full_ref.at[row_at(z), col_at(q)], z_send.at[d], z_recv.at[d], peer
+        )
+        for d, peer in enumerate(z_peers)
+    ]
+    own.start()
+    p_copies = [send(up_ref, full_ref.at[row_at(z), :], p_send, p_recv, partner)]
+    x_copies = []
+    for d in range(nz - 1):
+        z_copies[d].wait_recv()
+        piece = full_ref.at[row_at((z + nz - d - 1) % nz), col_at(q)]
+        for e in range(PLANE - 1):
+            n = d * (PLANE - 1) + e
+            x_copies.append(send(piece, piece, x_send.at[n], x_recv.at[n], mates[e]))
+        n = d * PLANE + PLANE - 1
+        p_copies.append(send(piece, piece, f_send.at[n], f_recv.at[n], partner))
+    for d in range(nz - 1):
+        for e in range(PLANE - 1):
+            x_copies[d * (PLANE - 1) + e].wait_recv()
+            piece = full_ref.at[row_at((z + nz - d - 1) % nz), col_at(mate(q, e + 1))]
+            n = d * PLANE + e
+            p_copies.append(send(piece, piece, f_send.at[n], f_recv.at[n], partner))
+    for copy in p_copies:
+        copy.wait_recv()
+    for copy in pending:
+        copy.wait_send()
+    own.wait()
+
+
+def gather_up(up_weight, n_fsdp):
+    rows, cols = up_weight.shape
+    nz = n_fsdp // 2
+    dma = pltpu.SemaphoreType.DMA
+    return pl.pallas_call(
+        functools.partial(gather_kernel, nz),
+        out_shape=jax.ShapeDtypeStruct((rows * n_fsdp, cols), up_weight.dtype),
+        in_specs=[pl.BlockSpec(memory_space=pl.ANY)],
+        out_specs=pl.BlockSpec(memory_space=pl.ANY),
+        scratch_shapes=[
+            dma,
+            dma((nz - 1,)),
+            dma((nz - 1,)),
+            dma,
+            dma,
+            dma(((nz - 1) * (PLANE - 1),)),
+            dma(((nz - 1) * (PLANE - 1),)),
+            dma(((nz - 1) * PLANE,)),
+            dma(((nz - 1) * PLANE,)),
+        ],
+        compiler_params=pltpu.CompilerParams(collective_id=0, has_side_effects=True),
+        name="gather_up",
+    )(up_weight)
+
+
+def mix_kernel(
+    n_dp, n_fsdp, width,
+    a_ref, h_ref, down_ref, proj_ref, gain_ref, emb_ref, all_ref,
+    ra, rh, s2, r2, s3, r3,
+    as_, ar, hs, hr, s2s, r2s, s3s, r3s, es, er, ps, pr,
+):
+    i = lax.axis_index("dp")
+    j = lax.axis_index("fsdp")
+    peers = [(j + d) % n_fsdp for d in range(1, n_fsdp)]
+    planes = [(i + e) % n_dp for e in range(1, n_dp)]
+    pass_rows, ff_rows = a_ref.shape[1:]
+    d_rows = h_ref.shape[2]
+    emb = proj_ref.shape[1]
+    group = n_fsdp * pass_rows
+    meet([(i, p) for p in peers] + [(p, j) for p in planes])
+    pending = []
+
+    def send(src, dst, ssem, rsem, device):
+        copy = remote(src, dst, ssem, rsem, device)
+        copy.start()
+        pending.append(copy)
+        return copy
+
+    first = []
+    second = []
+    for d, p in enumerate(peers):
+        first.append(send(a_ref.at[p], ra.at[j], as_.at[d], ar.at[d], (i, p)))
+        second.append(send(h_ref.at[p], rh.at[j], hs.at[d], hr.at[d], (i, p)))
+    ra[j] = a_ref[j]
+    rh[j] = h_ref[j]
+    for copy in first:
+        copy.wait_recv()
+    acts = ra[...].reshape(group, ff_rows)
+    parts = []
+    for d, p in enumerate(peers):
+        s2[d] = jnp.dot(acts, down_ref[p], preferred_element_type=jnp.float32).astype(s2.dtype)
+        parts.append(send(s2.at[d], r2.at[d], s2s.at[d], r2s.at[d], (i, p)))
+    pooled = jnp.dot(acts, down_ref[j], preferred_element_type=jnp.float32)
+    for copy in second:
+        copy.wait_recv()
+    pooled = pooled + rh[...].astype(jnp.float32).reshape(group, d_rows)
+    for d, copy in enumerate(parts):
+        copy.wait_recv()
+        pooled = pooled + r2[d].astype(jnp.float32)
+    squares = jnp.sum(pooled * pooled, axis=1, keepdims=True)
+    scaled = (pooled * gain_ref[...]).astype(proj_ref.dtype)
+    part = jnp.dot(scaled, proj_ref[...], preferred_element_type=jnp.float32)
+    s3[:, :, :emb] = part.astype(s3.dtype).reshape(n_fsdp, pass_rows, emb)
+    wide = jnp.broadcast_to(squares, (group, 128))
+    high = wide.astype(s3.dtype)
+    low = (wide - high.astype(jnp.float32)).astype(s3.dtype)
+    s3[:, :, emb : emb + 128] = high.reshape(n_fsdp, pass_rows, 128)
+    s3[:, :, emb + 128 : emb + 256] = low.reshape(n_fsdp, pass_rows, 128)
+    third = [
+        send(s3.at[p], r3.at[d], s3s.at[d], r3s.at[d], (i, p)) for d, p in enumerate(peers)
+    ]
+    total = s3[j].astype(jnp.float32)
+    for d, copy in enumerate(third):
+        copy.wait_recv()
+        total = total + r3[d].astype(jnp.float32)
+    norm = (total[:, emb : emb + 1] + total[:, emb + 128 : emb + 129]) / width
+    embedded = total[:, :emb] * lax.rsqrt(norm + EPSILON)
+    emb_ref[...] = embedded
+    all_ref[i, j] = embedded.astype(all_ref.dtype)
+    mine = all_ref.at[i, j]
+    fourth = [send(mine, mine, es.at[d], er.at[d], (i, p)) for d, p in enumerate(peers)]
+    for copy in fourth:
+        copy.wait_recv()
+    block = all_ref.at[i]
+    fifth = [send(block, block, ps.at[e], pr.at[e], (p, j)) for e, p in enumerate(planes)]
+    for copy in fifth:
+        copy.wait_recv()
+    for copy in pending:
+        copy.wait_send()
+
+
+def mix(acts, hid, down, proj, gain, n_dp):
+    n_fsdp, pass_rows, ff_rows = acts.shape
+    d_rows, emb = proj.shape
+    group = n_fsdp * pass_rows
+    bf = jnp.bfloat16
+    dma = pltpu.SemaphoreType.DMA
+    vmem = pl.BlockSpec(memory_space=pltpu.VMEM)
+    near = [dma((n_fsdp - 1,))] * 2
+    return pl.pallas_call(
+        functools.partial(mix_kernel, n_dp, n_fsdp, float(n_fsdp * d_rows)),
+        out_shape=(
+            jax.ShapeDtypeStruct((pass_rows, emb), jnp.float32),
+            jax.ShapeDtypeStruct((n_dp, n_fsdp, pass_rows, emb), bf),
+        ),
+        in_specs=[vmem] * 5,
+        out_specs=(vmem, vmem),
+        scratch_shapes=[
+            pltpu.VMEM((n_fsdp, pass_rows, ff_rows), bf),
+            pltpu.VMEM((n_fsdp, pass_rows, d_rows), bf),
+            pltpu.VMEM((n_fsdp - 1, group, d_rows), bf),
+            pltpu.VMEM((n_fsdp - 1, group, d_rows), bf),
+            pltpu.VMEM((n_fsdp, pass_rows, emb + 256), bf),
+            pltpu.VMEM((n_fsdp - 1, pass_rows, emb + 256), bf),
+        ]
+        + near * 5
+        + [dma((n_dp - 1,))] * 2,
+        compiler_params=pltpu.CompilerParams(
+            collective_id=1, has_side_effects=True, vmem_limit_bytes=40 * 1024 * 1024
+        ),
+        name="mix",
+    )(acts, hid, down, proj, gain)
 
 
 def on_device(hidden, lengths, norm_gain, up_weight, down_weight, pool_gain, proj_weight, owners):
@@ -34,7 +254,7 @@
     ).astype(jnp.bfloat16)
     hidden_pre = jnp.dot(
         normed,
-        lax.all_gather(up_weight, "fsdp", axis=0, tiled=True),
+        gather_up(up_weight, n_fsdp),
         preferred_element_type=jnp.float32,
     )
     activated = jax.nn.gelu(hidden_pre, approximate=True).astype(jnp.bfloat16)
@@ -46,29 +266,17 @@
     inverse = 1.0 / lengths.astype(jnp.float32)[:, None]
     act_mean = jnp.dot(inside, activated, preferred_element_type=jnp.float32) * inverse
     hid_mean = jnp.dot(inside, hidden, preferred_element_type=jnp.float32) * inverse
-    packed = jnp.concatenate(
-        [
-            act_mean.reshape(pass_rows, n_fsdp, ff_rows),
-            hid_mean.reshape(pass_rows, n_fsdp, d_rows),
-        ],
-        axis=2,
-    ).transpose(1, 0, 2)
-    pooled_in = exchange(packed).reshape(group, ff_rows + d_rows)
-    partial = fdot(pooled_in[:, :ff_rows], down_weight.astype(jnp.float32))
-    partial = partial.reshape(group, n_fsdp, d_rows).transpose(1, 0, 2)
-    pooled = jnp.sum(exchange(partial), axis=0) + pooled_in[:, ff_rows:]
-    squares = jnp.sum(pooled * pooled, axis=1, keepdims=True)
-    gain = lax.dynamic_slice(pool_gain, (me * d_rows,), (d_rows,))
-    emb_part = fdot(pooled * gain, proj_weight.astype(jnp.float32))
-    emb_part = jnp.concatenate([emb_part, jnp.broadcast_to(squares, (group, 128))], axis=1)
-    summed = jnp.sum(exchange(emb_part.reshape(n_fsdp, pass_rows, emb + 128)), axis=0)
-    embedded = summed[:, :emb] * lax.rsqrt(summed[:, emb : emb + 1] / width + EPSILON)
-    everyone = lax.all_gather(embedded, ("dp", "fsdp"), axis=0, tiled=True)
+    acts = act_mean.astype(jnp.bfloat16).reshape(pass_rows, n_fsdp, ff_rows).transpose(1, 0, 2)
+    hid = hid_mean.astype(jnp.bfloat16).reshape(pass_rows, n_fsdp, d_rows).transpose(1, 0, 2)
+    down = down_weight.reshape(ff_rows, n_fsdp, d_rows).transpose(1, 0, 2)
+    gain = lax.dynamic_slice(pool_gain, (me * d_rows,), (d_rows,))[None, :]
+    embedded, everyone = mix(acts, hid, down, proj_weight, gain, n_dp)
+    everyone = everyone.reshape(n_dp * group, emb)
     total_rows = float(everyone.shape[0])
-    average = jnp.sum(everyone, axis=0) / total_rows
+    average = jnp.sum(everyone.astype(jnp.float32), axis=0) / total_rows
     eye = jnp.eye(emb, dtype=jnp.float32)
     covariance = (
-        fdot(everyone.T, everyone) / total_rows
+        jnp.dot(everyone.T, everyone, preferred_element_type=jnp.float32) / total_rows
         - average[:, None] * average[None, :]
         + RIDGE_TERM * eye
     )

time: 256 us -> 140 us (0.55)
  waiting for transfers between devices: 167 us -> 0 us
  Pallas kernels: 0 us -> 104 us
  blocking collectives: 37.2 us -> 8.21 us
  between operations: 14.2 us -> 0.82 us
  matrix products: 28.1 us -> 21 us
  starting transfers between devices: 3.62 us -> 0 us
    all_gather x2 -> x0, waiting for transfers between devices: 146 us -> none  [the longest x1 92.1 us: on_device(): lax.all_gather(up_weight, 'fsdp', axis=0, tiled=True)]
    pallas_call x0 -> x2, Pallas kernels: none -> 104 us  [the longest x1 56.2 us: gather_up(): pl.pallas_call(functools.partial(gather_kernel, nz), out_shape=jax.ShapeD...]
    all_to_all x2 -> x0, blocking collectives: 29.9 us -> none  [exchange(): lax.all_to_all(blocks, 'fsdp', split_axis=0, concat_axis=0, tiled=True)]
    all_to_all x1 -> x0, waiting for transfers between devices: 19.9 us -> none  [exchange(): lax.all_to_all(blocks, 'fsdp', split_axis=0, concat_axis=0, tiled=True)]
    dot_general x10 -> x7, matrix products: 17.6 us -> 10.3 us  [fdot(): return jnp.dot(a, b, precision=HIGH, preferred_element_type=jnp.float32)]
    all_to_all x1 -> x0, starting transfers between devices: 3.55 us -> none  [exchange(): lax.all_to_all(blocks, 'fsdp', split_axis=0, concat_axis=0, tiled=True)]
  transfers between devices with their start and end apart: 3 -> 0, of which waited for: 3 -> 0; matrix products, arithmetic and copies ran while one was open for 2% -> 0% of each run, Pallas kernels for 0% -> 0%
where the time goes in v2:
time: 140 us
  Pallas kernels  104 us (74%)
  matrix products  21 us (15%)
  blocking collectives  8.21 us (6%)
  local copies, waits for them, and re-layouts  4.21 us (3%)
  other arithmetic  1.41 us (1%)
    pallas_call x1, Pallas kernels, gather_up(): pl.pallas_call(functools.partial(gather_kernel, nz), out_shape=jax.ShapeD...  56.2 us
    pallas_call x1, Pallas kernels, mix(): pl.pallas_call(functools.partial(mix_kernel, n_dp, n_fsdp, float(n_fsdp *...  47.9 us
    dot_general x7, matrix products, fdot(): return jnp.dot(a, b, precision=HIGH, preferred_element_type=jnp.float32)  10.3 us
    dot_general x1, matrix products, on_device(): jnp.dot(inside, activated, preferred_element_type=jnp.float32) * inverse  8.6 us
    all_to_all x1, blocking collectives, on_device(): lax.all_to_all(outgoing, 'dp', split_axis=0, concat_axis=0, tiled=True)  8.21 us

profile of v2, /device:TPU:0, one launch (start us, length us, event | category | flops | bytes accessed | tf_op | source)
XLA Modules:
  0.0 139.7 jit_solution(14877823257530969528)
XLA Ops:
  0.0 0.7 convert_divide_fusion
  0.7 56.2 %gather_up.1 = bf16[1536,3072]{1,0:T(8,128)(2,1)} custom-call(bf16[192,3072]{1,0:T(8,128)(2,1)} %up_ref.1), custom_call_target="tpu_custom_call" | custom-call | tf_op jit(solution)/shard_map/gather_up/pallas_call | solution.py:109
  56.9 0.0 copy-start.3
  56.9 0.4 fusion.9
  57.3 0.4 fusion.14
  57.6 8.6 %fusion.8 = bf16[16,3072]{1,0:T(8,128)(2,1)S(1)} fusion(bf16[1536,3072]{1,0:T(8,128)(2,1)} %gather_up.1, bf16[512,1536]{1,0:T(8,128)(2,1)S(1)} %copy-done.1, f32[1536]{0:T(1024)S(1)} %copy-done.3, f32[512]{0:T(512)S(1)} %add_rsqrt_fusion, f32[16]{0:T(128)S(1)} %convert_divide_fusion, s32[16]{0:T(128)S(1)} %copy-done.2, s32[512]{0:T(512)S(1)} %get-tuple-element.12, ...), kind=kOutput, calls=%fused_computation.12 | convolution fusion | flops 4899610624 | bytes 11125888 | tf_op jit(solution)/shard_map/dot_general | solution.py:267
  66.2 0.1 reshape.40
  66.4 1.7 %copy.15 = bf16[384,1536]{0,1:T(8,128)(2,1)S(1)} copy(bf16[384,1536]{1,0:T(8,128)(2,1)} %param.12) | data formatting | bytes 2359296 | tf_op args[4]
  68.2 0.9 copy.16
  69.1 0.8 dynamic_slice.3
  69.8 47.9 %mix.1 = (f32[16,768]{1,0:T(8,128)S(1)}, bf16[4,8,16,768]{3,2,1,0:T(8,128)(2,1)S(1)}) custom-call(bf16[8,16,384]{2,1,0:T(8,128)(2,1)S(1)} %bitcast.42, bf16[8,16,192]{2,1,0:T(8,128)(2,1)S(1)} %bitcast.43, bf16[8,384,192]{2,1,0:T(8,128)(2,1)S(1)} %bitcast.41, bf16[192,768]{1,0:T(8,128)(2,1)S(1)} %copy-done, f32[1,192]{1,0:T(1,128)S(1)} %bitcast.44), custom_call_target="tpu_custom_call" | custom-call | tf_op jit(solution)/shard_map/mix/pallas_call | solution.py:214
  117.8 0.2 convert_reduce_fusion
  117.9 1.7 %multiply_reduce_fusion = (f32[]{:T(128)}, f32[768,768]{1,0:T(8,128)S(1)}) fusion(f32[768]{0:T(1024)S(1)} %broadcast_multiply_fusion, bf16[4,8,16,768]{3,2,1,0:T(8,128)(2,1)S(1)} %get-tuple-element.8), kind=kOutput, calls=%fused_computation.20 | convolution fusion | flops 608698368 | bytes 3148804 | tf_op jit(solution)/shard_map/dot_general | solution.py:279
  120.3 3.2 %fusion.15 = f32[768,768]{1,0:T(8,128)S(1)} fusion(f32[768,768]{1,0:T(8,128)S(1)} %get-tuple-element.10, f32[]{:T(128)S(6)} %div.44), kind=kOutput, calls=%fused_computation.24 | convolution fusion | flops 2720268288 | bytes 4718596 | tf_op jit(solution)/shard_map/dot_general | solution.py:16
  123.5 3.1 %fusion.51 = f32[768,768]{1,0:T(8,128)S(1)} fusion(f32[768,768]{1,0:T(8,128)S(1)} %fusion.15), kind=kOutput, calls=%fused_computation.71 | convolution fusion | flops 2717908992 | bytes 4718592 | tf_op jit(solution)/shard_map/dot_general | solution.py:16
  126.6 0.8 fusion.29
  127.4 0.8 convolution_add_fusion.1
  128.2 0.8 convolution_add_fusion
  129.0 0.8 fusion.52
  129.8 0.8 fusion.31
  130.5 0.2 convert_reduce_fusion.1
  130.7 0.1 fusion.30
  130.9 8.2 %all_to_all.12 = bf16[4,8,768]{2,1,0:T(8,128)(2,1)S(1)} all-to-all(bf16[4,8,768]{2,1,0:T(8,128)(2,1)S(1)} %fusion.30), channel_id=1, replica_groups=mesh['dp'=4,'fsdp'=8] {'dp'}, dimensions={0} | all-to-all | bytes 98304 | tf_op jit(solution)/shard_map/all_to_all | solution.py:302
  139.1 0.6 copy.24
  (17 shorter events, 0.1 us)
Async XLA Ops:
  0.7 56.2 %copy-start.1 = (bf16[512,1536]{1,0:T(8,128)(2,1)S(1)}, bf16[512,1536]{1,0:T(8,128)(2,1)}, u32[]{:S(2)}) copy-start(bf16[512,1536]{1,0:T(8,128)(2,1)} %param.8) | copy-start | bytes 4718596
  0.7 56.6 %copy-start.2 = (s32[16]{0:T(128)S(1)}, s32[16]{0:T(128)}, u32[]{:S(2)}) copy-start(s32[16]{0:T(128)} %param.9) | copy-start | bytes 196
  56.9 0.8 copy-start.3
  66.4 3.4 %copy-start = (bf16[192,768]{1,0:T(8,128)(2,1)S(1)}, bf16[192,768]{1,0:T(8,128)(2,1)}, u32[]{:S(2)}) copy-start(bf16[192,768]{1,0:T(8,128)(2,1)} %proj_ref.1) | copy-start | bytes 884740
  129.0 1.6 %copy-start.4 = (s32[16,1]{0,1:T(1,128)S(1)}, s32[16,1]{0,1:T(1,128)}, u32[]{:S(2)}) copy-start(s32[16,1]{0,1:T(1,128)} %param.15) | copy-start | bytes 196

commit v3 on v2

--- a/solution.py
+++ b/solution.py
@@ -61,7 +61,7 @@
 
     partner = (i, z * 2 + 1 - c)
     z_peers = [(i, ((z + d) % nz) * 2 + c) for d in range(1, nz)]
-    mates = [(base + mate(q, e), j) for e in range(1, PLANE)]
+    mates = [(base + mate(q, e), j) for e in range(1, 3)]
     meet([partner] + z_peers + mates)
     own = pltpu.make_async_copy(up_ref, full_ref.at[row_at(z), :], own_sem)
     pending = []
@@ -80,21 +80,38 @@
     ]
     own.start()
     p_copies = [send(up_ref, full_ref.at[row_at(z), :], p_send, p_recv, partner)]
-    x_copies = []
-    for d in range(nz - 1):
+    near_x, near_y = mates[0], mates[1]
+    half = rows // 2
+
+    def half_at(level, part):
+        return pl.ds(pl.multiple_of((level * 2 + c) * rows + part * half, half), half)
+
+    def forward(piece, n):
+        p_copies.append(send(piece, piece, f_send.at[n], f_recv.at[n], partner))
+
+    levels = [(z + nz - d - 1) % nz for d in range(nz - 1)]
+    direct = []
+    for d, level in enumerate(levels):
         z_copies[d].wait_recv()
-        piece = full_ref.at[row_at((z + nz - d - 1) % nz), col_at(q)]
-        for e in range(PLANE - 1):
-            n = d * (PLANE - 1) + e
-            x_copies.append(send(piece, piece, x_send.at[n], x_recv.at[n], mates[e]))
-        n = d * PLANE + PLANE - 1
-        p_copies.append(send(piece, piece, f_send.at[n], f_recv.at[n], partner))
-    for d in range(nz - 1):
-        for e in range(PLANE - 1):
-            x_copies[d * (PLANE - 1) + e].wait_recv()
-            piece = full_ref.at[row_at((z + nz - d - 1) % nz), col_at(mate(q, e + 1))]
-            n = d * PLANE + e
-            p_copies.append(send(piece, piece, f_send.at[n], f_recv.at[n], partner))
+        piece = full_ref.at[row_at(level), col_at(q)]
+        for e in range(2):
+            n = d * 4 + e
+            direct.append(send(piece, piece, x_send.at[n], x_recv.at[n], mates[e]))
+        forward(piece, d * 5)
+    relays = []
+    for d, level in enumerate(levels):
+        for e in range(2):
+            direct[d * 2 + e].wait_recv()
+            side = col_at(mate(q, e + 1))
+            piece = full_ref.at[half_at(level, e), side]
+            n = d * 4 + 2 + e
+            to = near_y if e == 0 else near_x
+            relays.append(send(piece, piece, x_send.at[n], x_recv.at[n], to))
+            forward(full_ref.at[row_at(level), side], d * 5 + 1 + e)
+    for d, level in enumerate(levels):
+        for e in range(2):
+            relays[d * 2 + e].wait_recv()
+            forward(full_ref.at[half_at(level, e), col_at(mate(q, 3))], d * 5 + 3 + e)
     for copy in p_copies:
         copy.wait_recv()
     for copy in pending:
@@ -117,10 +134,10 @@
             dma((nz - 1,)),
             dma,
             dma,
-            dma(((nz - 1) * (PLANE - 1),)),
-            dma(((nz - 1) * (PLANE - 1),)),
-            dma(((nz - 1) * PLANE,)),
-            dma(((nz - 1) * PLANE,)),
+            dma(((nz - 1) * 4,)),
+            dma(((nz - 1) * 4,)),
+            dma(((nz - 1) * 5,)),
+            dma(((nz - 1) * 5,)),
         ],
         compiler_params=pltpu.CompilerParams(collective_id=0, has_side_effects=True),
         name="gather_up",
@@ -130,17 +147,23 @@
 def mix_kernel(
     n_dp, n_fsdp, width,
     a_ref, h_ref, down_ref, proj_ref, gain_ref, emb_ref, all_ref,
-    ra, rh, s2, r2, s3, r3,
-    as_, ar, hs, hr, s2s, r2s, s3s, r3s, es, er, ps, pr,
+    ra, rh, pj, sp, rp, s2, r2, s3, r3,
+    as_, ar, hs, hr, s2s, r2s, s3s, r3s, es, er, ps, pr, qs, qr, cs, cr,
 ):
     i = lax.axis_index("dp")
     j = lax.axis_index("fsdp")
+    nz = n_fsdp // 2
+    z = j // 2
+    c = j % 2
+    partner = (i, z * 2 + 1 - c)
     peers = [(j + d) % n_fsdp for d in range(1, n_fsdp)]
+    levels = [(z + d) % nz for d in range(1, nz)]
     planes = [(i + e) % n_dp for e in range(1, n_dp)]
     pass_rows, ff_rows = a_ref.shape[1:]
-    d_rows = h_ref.shape[2]
+    cols = h_ref.shape[2]
     emb = proj_ref.shape[1]
-    group = n_fsdp * pass_rows
+    half = nz * pass_rows
+    slot = c * nz + z
     meet([(i, p) for p in peers] + [(p, j) for p in planes])
     pending = []
 
@@ -150,54 +173,77 @@
         pending.append(copy)
         return copy
 
+    def along(level):
+        return (i, level * 2 + c)
+
     first = []
+    for d, p in enumerate(peers):
+        first.append(send(a_ref.at[p], ra.at[slot], as_.at[d], ar.at[d], (i, p)))
     second = []
-    for d, p in enumerate(peers):
-        first.append(send(a_ref.at[p], ra.at[j], as_.at[d], ar.at[d], (i, p)))
-        second.append(send(h_ref.at[p], rh.at[j], hs.at[d], hr.at[d], (i, p)))
-    ra[j] = a_ref[j]
-    rh[j] = h_ref[j]
+    for d, v in enumerate(levels):
+        second.append(send(h_ref.at[v], rh.at[z], hs.at[d], hr.at[d], along(v)))
+    proj_copy = send(proj_ref, pj.at[c], cs.at[0], cr.at[0], partner)
+    pj[c] = proj_ref[...]
+    ra[slot] = a_ref[j]
+    rh[z] = h_ref[z]
     for copy in first:
         copy.wait_recv()
-    acts = ra[...].reshape(group, ff_rows)
-    parts = []
-    for d, p in enumerate(peers):
-        s2[d] = jnp.dot(acts, down_ref[p], preferred_element_type=jnp.float32).astype(s2.dtype)
-        parts.append(send(s2.at[d], r2.at[d], s2s.at[d], r2s.at[d], (i, p)))
-    pooled = jnp.dot(acts, down_ref[j], preferred_element_type=jnp.float32)
+
+    def share(core):
+        rows = ra[pl.ds(core * nz, nz)].reshape(half, ff_rows)
+        return jnp.dot(rows, down_ref[...], preferred_element_type=jnp.float32)
+
+    sp[...] = share(1 - c).astype(sp.dtype)
+    swap = send(sp, rp, cs.at[1], cr.at[1], partner)
+    mine = share(c)
+    swap.wait_recv()
+    mine = mine + rp[...].astype(jnp.float32)
+    for v in range(nz):
+        s2[v] = mine[:, v * cols : (v + 1) * cols].astype(s2.dtype)
+    parts = [
+        send(s2.at[v], r2.at[d], s2s.at[d], r2s.at[d], along(v)) for d, v in enumerate(levels)
+    ]
     for copy in second:
         copy.wait_recv()
-    pooled = pooled + rh[...].astype(jnp.float32).reshape(group, d_rows)
+    pooled = s2[z].astype(jnp.float32) + rh[...].astype(jnp.float32).reshape(half, cols)
+    proj_copy.wait_recv()
     for d, copy in enumerate(parts):
         copy.wait_recv()
         pooled = pooled + r2[d].astype(jnp.float32)
     squares = jnp.sum(pooled * pooled, axis=1, keepdims=True)
     scaled = (pooled * gain_ref[...]).astype(proj_ref.dtype)
-    part = jnp.dot(scaled, proj_ref[...], preferred_element_type=jnp.float32)
-    s3[:, :, :emb] = part.astype(s3.dtype).reshape(n_fsdp, pass_rows, emb)
-    wide = jnp.broadcast_to(squares, (group, 128))
+    part = jnp.dot(scaled, pj[...].reshape(cols, emb), preferred_element_type=jnp.float32)
+    s3[:, :, :emb] = part.astype(s3.dtype).reshape(nz, pass_rows, emb)
+    wide = jnp.broadcast_to(squares, (half, 128))
     high = wide.astype(s3.dtype)
     low = (wide - high.astype(jnp.float32)).astype(s3.dtype)
-    s3[:, :, emb : emb + 128] = high.reshape(n_fsdp, pass_rows, 128)
-    s3[:, :, emb + 128 : emb + 256] = low.reshape(n_fsdp, pass_rows, 128)
+    s3[:, :, emb : emb + 128] = high.reshape(nz, pass_rows, 128)
+    s3[:, :, emb + 128 : emb + 256] = low.reshape(nz, pass_rows, 128)
     third = [
-        send(s3.at[p], r3.at[d], s3s.at[d], r3s.at[d], (i, p)) for d, p in enumerate(peers)
+        send(s3.at[v], r3.at[d], s3s.at[d], r3s.at[d], along(v)) for d, v in enumerate(levels)
     ]
-    total = s3[j].astype(jnp.float32)
+    total = s3[z].astype(jnp.float32)
     for d, copy in enumerate(third):
         copy.wait_recv()
         total = total + r3[d].astype(jnp.float32)
     norm = (total[:, emb : emb + 1] + total[:, emb + 128 : emb + 129]) / width
     embedded = total[:, :emb] * lax.rsqrt(norm + EPSILON)
     emb_ref[...] = embedded
-    all_ref[i, j] = embedded.astype(all_ref.dtype)
-    mine = all_ref.at[i, j]
-    fourth = [send(mine, mine, es.at[d], er.at[d], (i, p)) for d, p in enumerate(peers)]
+    all_ref[i, c, z] = embedded.astype(all_ref.dtype)
+    mine_rows = all_ref.at[i, c, z]
+    fourth = [
+        send(mine_rows, mine_rows, es.at[d], er.at[d], along(v)) for d, v in enumerate(levels)
+    ]
     for copy in fourth:
         copy.wait_recv()
-    block = all_ref.at[i]
+    block = all_ref.at[i, c]
     fifth = [send(block, block, ps.at[e], pr.at[e], (p, j)) for e, p in enumerate(planes)]
-    for copy in fifth:
+    last = [send(block, block, qs.at[0], qr.at[0], partner)]
+    for e, copy in enumerate(fifth):
+        copy.wait_recv()
+        piece = all_ref.at[(i + n_dp - e - 1) % n_dp, c]
+        last.append(send(piece, piece, qs.at[e + 1], qr.at[e + 1], partner))
+    for copy in last:
         copy.wait_recv()
     for copy in pending:
         copy.wait_send()
@@ -205,30 +251,38 @@
 
 def mix(acts, hid, down, proj, gain, n_dp):
     n_fsdp, pass_rows, ff_rows = acts.shape
+    nz = n_fsdp // 2
     d_rows, emb = proj.shape
-    group = n_fsdp * pass_rows
+    cols = 2 * d_rows
+    half = nz * pass_rows
+    width = down.shape[1]
     bf = jnp.bfloat16
     dma = pltpu.SemaphoreType.DMA
     vmem = pl.BlockSpec(memory_space=pltpu.VMEM)
-    near = [dma((n_fsdp - 1,))] * 2
     return pl.pallas_call(
-        functools.partial(mix_kernel, n_dp, n_fsdp, float(n_fsdp * d_rows)),
+        functools.partial(mix_kernel, n_dp, n_fsdp, float(width)),
         out_shape=(
             jax.ShapeDtypeStruct((pass_rows, emb), jnp.float32),
-            jax.ShapeDtypeStruct((n_dp, n_fsdp, pass_rows, emb), bf),
+            jax.ShapeDtypeStruct((n_dp, 2, nz, pass_rows, emb), bf),
         ),
         in_specs=[vmem] * 5,
         out_specs=(vmem, vmem),
         scratch_shapes=[
             pltpu.VMEM((n_fsdp, pass_rows, ff_rows), bf),
-            pltpu.VMEM((n_fsdp, pass_rows, d_rows), bf),
-            pltpu.VMEM((n_fsdp - 1, group, d_rows), bf),
-            pltpu.VMEM((n_fsdp - 1, group, d_rows), bf),
-            pltpu.VMEM((n_fsdp, pass_rows, emb + 256), bf),
-            pltpu.VMEM((n_fsdp - 1, pass_rows, emb + 256), bf),
+            pltpu.VMEM((nz, pass_rows, cols), bf),
+            pltpu.VMEM((2, d_rows, emb), bf),
+            pltpu.VMEM((half, width), bf),
+            pltpu.VMEM((half, width), bf),
+            pltpu.VMEM((nz, half, cols), bf),
+            pltpu.VMEM((nz - 1, half, cols), bf),
+            pltpu.VMEM((nz, pass_rows, emb + 256), bf),
+            pltpu.VMEM((nz - 1, pass_rows, emb + 256), bf),
         ]
-        + near * 5
-        + [dma((n_dp - 1,))] * 2,
+        + [dma((n_fsdp - 1,))] * 2
+        + [dma((nz - 1,))] * 8
+        + [dma((n_dp - 1,))] * 2
+        + [dma((n_dp,))] * 2
+        + [dma((2,))] * 2,
         compiler_params=pltpu.CompilerParams(
             collective_id=1, has_side_effects=True, vmem_limit_bytes=40 * 1024 * 1024
         ),
@@ -267,10 +321,10 @@
     act_mean = jnp.dot(inside, activated, preferred_element_type=jnp.float32) * inverse
     hid_mean = jnp.dot(inside, hidden, preferred_element_type=jnp.float32) * inverse
     acts = act_mean.astype(jnp.bfloat16).reshape(pass_rows, n_fsdp, ff_rows).transpose(1, 0, 2)
-    hid = hid_mean.astype(jnp.bfloat16).reshape(pass_rows, n_fsdp, d_rows).transpose(1, 0, 2)
-    down = down_weight.reshape(ff_rows, n_fsdp, d_rows).transpose(1, 0, 2)
-    gain = lax.dynamic_slice(pool_gain, (me * d_rows,), (d_rows,))[None, :]
-    embedded, everyone = mix(acts, hid, down, proj_weight, gain, n_dp)
+    nz = n_fsdp // 2
+    hid = hid_mean.astype(jnp.bfloat16).reshape(pass_rows, nz, 2 * d_rows).transpose(1, 0, 2)
+    gain = lax.dynamic_slice(pool_gain, (me // 2 * 2 * d_rows,), (2 * d_rows,))[None, :]
+    embedded, everyone = mix(acts, hid, down_weight, proj_weight, gain, n_dp)
     everyone = everyone.reshape(n_dp * group, emb)
     total_rows = float(everyone.shape[0])
     average = jnp.sum(everyone.astype(jnp.float32), axis=0) / total_rows

time: 140 us -> 123 us (0.88)
  Pallas kernels: 104 us -> 87.1 us
  matrix products: 21 us -> 25 us
  local copies, waits for them, and re-layouts: 4.21 us -> 1.46 us
    pallas_call x1, Pallas kernels: 47.9 us -> 35.6 us  [mix(): pl.pallas_call(functools.partial(mix_kernel, n_dp, n_fsdp, float(width)),...]
    pallas_call x1, Pallas kernels: 56.2 us -> 51.5 us  [gather_up(): pl.pallas_call(functools.partial(gather_kernel, nz), out_shape=jax.ShapeD...]
    dot_general x7, matrix products: 10.3 us -> 12.8 us  [fdot(): return jnp.dot(a, b, precision=HIGH, preferred_element_type=jnp.float32)]
    unnamed x12 -> x15, local copies, waits for them, and re-layouts: 2.39 us -> 0.66 us
where the time goes in v3:
time: 123 us; the launch traced here: 122 us
  Pallas kernels  87.1 us (71%)
  matrix products  25 us (20%)
  blocking collectives  7.29 us (6%)
  local copies, waits for them, and re-layouts  1.46 us (1%)
    pallas_call x1, Pallas kernels, gather_up(): pl.pallas_call(functools.partial(gather_kernel, nz), out_shape=jax.ShapeD...  51.5 us
    pallas_call x1, Pallas kernels, mix(): pl.pallas_call(functools.partial(mix_kernel, n_dp, n_fsdp, float(width)),...  35.6 us
    dot_general x7, matrix products, fdot(): return jnp.dot(a, b, precision=HIGH, preferred_element_type=jnp.float32)  12.8 us
    dot_general x1, matrix products, on_device(): jnp.dot(inside, activated, preferred_element_type=jnp.float32) * inverse  8.8 us
    all_to_all x1, blocking collectives, on_device(): lax.all_to_all(outgoing, 'dp', split_axis=0, concat_axis=0, tiled=True)  7.29 us
    dot_general x1, matrix products, on_device(): jnp.dot(everyone.T, everyone, preferred_element_type=jnp.float32)  2.86 us

profile of v3, /device:TPU:0, one launch (start us, length us, event | category | flops | bytes accessed | tf_op | source)
XLA Modules:
  0.0 122.5 jit_solution(1085633275660050361)
XLA Ops:
  0.0 0.0 copy-start.2
  0.0 0.0 copy-start.4
  0.0 51.5 %gather_up.1 = bf16[1536,3072]{1,0:T(8,128)(2,1)} custom-call(bf16[192,3072]{1,0:T(8,128)(2,1)} %up_ref.1), custom_call_target="tpu_custom_call" | custom-call | tf_op jit(solution)/shard_map/gather_up/pallas_call | solution.py:126
  51.6 0.0 copy-start.5
  51.6 0.4 fusion.9
  52.0 0.4 fusion.14
  52.4 0.0 copy-start
  52.4 0.0 copy-start.1
  52.4 8.8 %fusion.8 = bf16[16,3072]{1,0:T(8,128)(2,1)S(1)} fusion(bf16[1536,3072]{1,0:T(8,128)(2,1)} %gather_up.1, bf16[512,1536]{1,0:T(8,128)(2,1)S(1)} %copy-done.2, f32[1536]{0:T(1024)S(1)} %copy-done.5, f32[512]{0:T(512)S(1)} %add_rsqrt_fusion, f32[16]{0:T(128)S(1)} %convert_divide_fusion, s32[16]{0:T(128)S(1)} %copy-done.4, s32[512]{0:T(512)S(1)} %get-tuple-element.12, ...), kind=kOutput, calls=%fused_computation.12 | convolution fusion | flops 4899610624 | bytes 11125888 | tf_op jit(solution)/shard_map/dot_general | solution.py:321
  61.2 0.8 dynamic_slice.3
  62.0 35.6 %mix.1 = (f32[16,768]{1,0:T(8,128)S(1)}, bf16[4,2,4,16,768]{4,3,2,1,0:T(8,128)(2,1)S(1)}) custom-call(bf16[8,16,384]{2,1,0:T(8,128)(2,1)S(1)} %bitcast.42, bf16[4,16,384]{2,1,0:T(8,128)(2,1)S(1)} %bitcast.43, bf16[384,1536]{1,0:T(8,128)(2,1)S(1)} %copy-done, bf16[192,768]{1,0:T(8,128)(2,1)S(1)} %copy-done.1, f32[1,384]{1,0:T(1,128)S(1)} %broadcast_in_dim.2.gain_ref), custom_call_target="tpu_custom_call" | custom-call | tf_op jit(solution)/shard_map/mix/pallas_call | solution.py:262
  97.7 0.2 convert_reduce_fusion
  97.8 2.9 %multiply_reduce_fusion = (f32[]{:T(128)}, f32[768,768]{1,0:T(8,128)}) fusion(f32[768]{0:T(1024)S(1)} %broadcast_multiply_fusion, bf16[4,2,4,16,768]{4,3,2,1,0:T(8,128)(2,1)S(1)} %get-tuple-element.8), kind=kOutput, calls=%fused_computation.20 | convolution fusion | flops 608698368 | bytes 3148804 | tf_op jit(solution)/shard_map/dot_general | solution.py:333
  101.4 5.7 %fusion.15 = f32[768,768]{1,0:T(8,128)S(1)} fusion(f32[768,768]{1,0:T(8,128)} %get-tuple-element.10, f32[]{:T(128)S(6)} %div.55), kind=kOutput, calls=%fused_computation.24 | convolution fusion | flops 2720268288 | bytes 4718596 | tf_op jit(solution)/shard_map/dot_general | solution.py:16
  107.1 0.9 fusion.29
  108.0 3.1 %fusion.51 = f32[768,768]{1,0:T(8,128)S(1)} fusion(f32[768,768]{1,0:T(8,128)S(1)} %fusion.15), kind=kOutput, calls=%fused_computation.71 | convolution fusion | flops 2717908992 | bytes 4718592 | tf_op jit(solution)/shard_map/dot_general | solution.py:16
  111.1 0.8 convolution_add_fusion.1
  111.9 0.8 convolution_add_fusion
  112.7 0.8 fusion.52
  113.5 0.8 fusion.31
  114.2 0.2 convert_reduce_fusion.1
  114.4 0.1 fusion.30
  114.6 7.3 %all_to_all.12 = bf16[4,8,768]{2,1,0:T(8,128)(2,1)S(1)} all-to-all(bf16[4,8,768]{2,1,0:T(8,128)(2,1)S(1)} %fusion.30), channel_id=1, replica_groups=mesh['dp'=4,'fsdp'=8] {'dp'}, dimensions={0} | all-to-all | bytes 98304 | tf_op jit(solution)/shard_map/all_to_all | solution.py:356
  121.9 0.6 copy.21
  (19 shorter events, 0.1 us)
Async XLA Ops:
  0.0 51.5 %copy-start.2 = (bf16[512,1536]{1,0:T(8,128)(2,1)S(1)}, bf16[512,1536]{1,0:T(8,128)(2,1)}, u32[]{:S(2)}) copy-start(bf16[512,1536]{1,0:T(8,128)(2,1)} %param.8) | copy-start | bytes 4718596
  0.0 51.9 %copy-start.4 = (s32[16]{0:T(128)S(1)}, s32[16]{0:T(128)}, u32[]{:S(2)}) copy-start(s32[16]{0:T(128)} %param.9) | copy-start | bytes 196
  51.6 0.8 copy-start.5
  52.4 9.7 %copy-start = (bf16[384,1536]{1,0:T(8,128)(2,1)S(1)}, bf16[384,1536]{1,0:T(8,128)(2,1)}, u32[]{:S(2)}) copy-start(bf16[384,1536]{1,0:T(8,128)(2,1)} %down_ref.1) | copy-start | bytes 3538948
  52.4 9.7 %copy-start.1 = (bf16[192,768]{1,0:T(8,128)(2,1)S(1)}, bf16[192,768]{1,0:T(8,128)(2,1)}, u32[]{:S(2)}) copy-start(bf16[192,768]{1,0:T(8,128)(2,1)} %proj_ref.1) | copy-start | bytes 884740
  101.4 5.8 %copy-start.3 = (f32[768,768]{1,0:T(8,128)S(1)}, f32[768,768]{1,0:T(8,128)}, u32[]{:S(2)}) copy-start(f32[768,768]{1,0:T(8,128)} %get-tuple-element.10) | copy-start | bytes 7077892
  112.7 1.6 %copy-start.6 = (s32[16,1]{0,1:T(1,128)S(1)}, s32[16,1]{0,1:T(1,128)}, u32[]{:S(2)}) copy-start(s32[16,1]{0,1:T(1,128)} %param.15) | copy-start | bytes 196

commit v4 on v3

--- a/solution.py
+++ b/solution.py
@@ -18,6 +18,7 @@
 
 MESH = pl.DeviceIdType.MESH
 PLANE = 4
+CHUNKS = 3
 
 
 def remote(src, dst, send, recv, device):
@@ -72,46 +73,73 @@
         pending.append(copy)
         return copy
 
-    z_copies = [
-        send(
-            up_ref.at[:, col_at(q)], full_ref.at[row_at(z), col_at(q)], z_send.at[d], z_recv.at[d], peer
-        )
-        for d, peer in enumerate(z_peers)
-    ]
-    own.start()
-    p_copies = [send(up_ref, full_ref.at[row_at(z), :], p_send, p_recv, partner)]
     near_x, near_y = mates[0], mates[1]
     half = rows // 2
+    chunk = cols // CHUNKS
 
     def half_at(level, part):
         return pl.ds(pl.multiple_of((level * 2 + c) * rows + part * half, half), half)
 
+    def chunk_at(part, ch):
+        return pl.ds(pl.multiple_of(part * cols + ch * chunk, chunk), chunk)
+
+    z_copies = {}
+    direct = {}
+    relays = {}
+    p_copies = []
+
+    def start_z(ch):
+        for d, peer in enumerate(z_peers):
+            n = ch * (nz - 1) + d
+            src = up_ref.at[:, chunk_at(q, ch)]
+            dst = full_ref.at[row_at(z), chunk_at(q, ch)]
+            z_copies[ch, d] = send(src, dst, z_send.at[n], z_recv.at[n], peer)
+
     def forward(piece, n):
         p_copies.append(send(piece, piece, f_send.at[n], f_recv.at[n], partner))
 
     levels = [(z + nz - d - 1) % nz for d in range(nz - 1)]
-    direct = []
-    for d, level in enumerate(levels):
-        z_copies[d].wait_recv()
-        piece = full_ref.at[row_at(level), col_at(q)]
-        for e in range(2):
-            n = d * 4 + e
-            direct.append(send(piece, piece, x_send.at[n], x_recv.at[n], mates[e]))
-        forward(piece, d * 5)
-    relays = []
-    for d, level in enumerate(levels):
-        for e in range(2):
-            direct[d * 2 + e].wait_recv()
-            side = col_at(mate(q, e + 1))
-            piece = full_ref.at[half_at(level, e), side]
-            n = d * 4 + 2 + e
-            to = near_y if e == 0 else near_x
-            relays.append(send(piece, piece, x_send.at[n], x_recv.at[n], to))
-            forward(full_ref.at[row_at(level), side], d * 5 + 1 + e)
-    for d, level in enumerate(levels):
-        for e in range(2):
-            relays[d * 2 + e].wait_recv()
-            forward(full_ref.at[half_at(level, e), col_at(mate(q, 3))], d * 5 + 3 + e)
+
+    def spread(ch):
+        for d, level in enumerate(levels):
+            z_copies[ch, d].wait_recv()
+            piece = full_ref.at[row_at(level), chunk_at(q, ch)]
+            for e in range(2):
+                n = (ch * (nz - 1) + d) * 4 + e
+                direct[ch, d, e] = send(piece, piece, x_send.at[n], x_recv.at[n], mates[e])
+            forward(piece, (ch * (nz - 1) + d) * 5)
+        if ch + 2 < CHUNKS:
+            start_z(ch + 2)
+
+    def relay(ch):
+        for d, level in enumerate(levels):
+            for e in range(2):
+                direct[ch, d, e].wait_recv()
+                side = chunk_at(mate(q, e + 1), ch)
+                piece = full_ref.at[half_at(level, e), side]
+                n = (ch * (nz - 1) + d) * 4 + 2 + e
+                to = near_y if e == 0 else near_x
+                relays[ch, d, e] = send(piece, piece, x_send.at[n], x_recv.at[n], to)
+                forward(full_ref.at[row_at(level), side], (ch * (nz - 1) + d) * 5 + 1 + e)
+
+    def finish(ch):
+        for d, level in enumerate(levels):
+            for e in range(2):
+                relays[ch, d, e].wait_recv()
+                piece = full_ref.at[half_at(level, e), chunk_at(mate(q, 3), ch)]
+                forward(piece, (ch * (nz - 1) + d) * 5 + 3 + e)
+
+    start_z(0)
+    start_z(1)
+    own.start()
+    p_copies.append(send(up_ref, full_ref.at[row_at(z), :], p_send, p_recv, partner))
+    for step in range(CHUNKS + 2):
+        if step < CHUNKS:
+            spread(step)
+        if 0 <= step - 1 < CHUNKS:
+            relay(step - 1)
+        if step >= 2:
+            finish(step - 2)
     for copy in p_copies:
         copy.wait_recv()
     for copy in pending:
@@ -130,14 +158,14 @@
         out_specs=pl.BlockSpec(memory_space=pl.ANY),
         scratch_shapes=[
             dma,
-            dma((nz - 1,)),
-            dma((nz - 1,)),
+            dma((CHUNKS * (nz - 1),)),
+            dma((CHUNKS * (nz - 1),)),
             dma,
             dma,
-            dma(((nz - 1) * 4,)),
-            dma(((nz - 1) * 4,)),
-            dma(((nz - 1) * 5,)),
-            dma(((nz - 1) * 5,)),
+            dma((CHUNKS * (nz - 1) * 4,)),
+            dma((CHUNKS * (nz - 1) * 4,)),
+            dma((CHUNKS * (nz - 1) * 5,)),
+            dma((CHUNKS * (nz - 1) * 5,)),
         ],
         compiler_params=pltpu.CompilerParams(collective_id=0, has_side_effects=True),
         name="gather_up",
@@ -288,6 +316,34 @@
         ),
         name="mix",
     )(acts, hid, down, proj, gain)
+
+
+def route_kernel(n_dp, out_ref, in_ref, ssem, rsem):
+    i = lax.axis_index("dp")
+    j = lax.axis_index("fsdp")
+    planes = [(i + e) % n_dp for e in range(1, n_dp)]
+    meet([(p, j) for p in planes])
+    copies = []
+    for e, p in enumerate(planes):
+        copy = remote(out_ref.at[p], in_ref.at[i], ssem.at[e], rsem.at[e], (p, j))
+        copy.start()
+        copies.append(copy)
+    in_ref[i] = out_ref[i]
+    for copy in copies:
+        copy.wait()
+
+
+def route(outgoing, n_dp):
+    vmem = pl.BlockSpec(memory_space=pltpu.VMEM)
+    return pl.pallas_call(
+        functools.partial(route_kernel, n_dp),
+        out_shape=jax.ShapeDtypeStruct(outgoing.shape, outgoing.dtype),
+        in_specs=[vmem],
+        out_specs=vmem,
+        scratch_shapes=[pltpu.SemaphoreType.DMA((n_dp - 1,))] * 2,
+        compiler_params=pltpu.CompilerParams(collective_id=2, has_side_effects=True),
+        name="route",
+    )(outgoing)
 
 
 def on_device(hidden, lengths, norm_gain, up_weight, down_weight, pool_gain, proj_weight, owners):
@@ -353,7 +409,8 @@
     slot_index = lax.broadcasted_iota(jnp.int32, (n_dp * capacity, pass_rows), 0)
     selector = (slot_index == target[None, :]).astype(jnp.bfloat16)
     outgoing = jnp.dot(selector, whitened, preferred_element_type=jnp.float32).astype(jnp.bfloat16)
-    return lax.all_to_all(outgoing, "dp", split_axis=0, concat_axis=0, tiled=True)
+    owned = route(outgoing.reshape(n_dp, capacity, emb), n_dp)
+    return owned.reshape(n_dp * capacity, emb)
 
 
 def solution(mesh):

time: 123 us -> 117 us (0.951)
  blocking collectives: 7.29 us -> 0 us
    all_to_all x1 -> x0, blocking collectives: 7.29 us -> none  [on_device(): lax.all_to_all(outgoing, 'dp', split_axis=0, concat_axis=0, tiled=True)]
    pallas_call x0 -> x1, Pallas kernels: none -> 6.07 us  [route(): pl.pallas_call(functools.partial(route_kernel, n_dp), out_shape=jax.Shape...]
    pallas_call x1, Pallas kernels: 35.6 us -> 32.3 us  [mix(): pl.pallas_call(functools.partial(mix_kernel, n_dp, n_fsdp, float(width)),...]
    pallas_call x1, Pallas kernels: 51.5 us -> 49.3 us  [gather_up(): pl.pallas_call(functools.partial(gather_kernel, nz), out_shape=jax.ShapeD...]
where the time goes in v4:
time: 117 us; the launch traced here: 116 us
  Pallas kernels  87.6 us (75%)
  matrix products  24.8 us (21%)
  local copies, waits for them, and re-layouts  2.32 us (2%)
    pallas_call x1, Pallas kernels, gather_up(): pl.pallas_call(functools.partial(gather_kernel, nz), out_shape=jax.ShapeD...  49.3 us
    pallas_call x1, Pallas kernels, mix(): pl.pallas_call(functools.partial(mix_kernel, n_dp, n_fsdp, float(width)),...  32.3 us
    dot_general x7, matrix products, fdot(): return jnp.dot(a, b, precision=HIGH, preferred_element_type=jnp.float32)  12.1 us
    dot_general x1, matrix products, on_device(): jnp.dot(inside, activated, preferred_element_type=jnp.float32) * inverse  8.73 us
    pallas_call x1, Pallas kernels, route(): pl.pallas_call(functools.partial(route_kernel, n_dp), out_shape=jax.Shape...  6.07 us
    dot_general x1, matrix products, on_device(): jnp.dot(everyone.T, everyone, preferred_element_type=jnp.float32)  2.86 us

profile of v4, /device:TPU:0, one launch (start us, length us, event | category | flops | bytes accessed | tf_op | source)
XLA Modules:
  0.0 116.4 jit_solution(4759381509857115012)
XLA Ops:
  0.0 49.3 %gather_up.1 = bf16[1536,3072]{1,0:T(8,128)(2,1)} custom-call(bf16[192,3072]{1,0:T(8,128)(2,1)} %up_ref.1), custom_call_target="tpu_custom_call" | custom-call | tf_op jit(solution)/shard_map/gather_up/pallas_call | solution.py:154
  49.3 0.4 fusion.9
  49.7 0.0 copy-start.1
  49.8 8.7 %fusion.8 = bf16[16,3072]{1,0:T(8,128)(2,1)S(1)} fusion(bf16[1536,3072]{1,0:T(8,128)(2,1)} %gather_up.1, bf16[512,1536]{1,0:T(8,128)(2,1)S(1)} %copy-done.2, f32[1536]{0:T(1024)S(1)} %copy-done.5, f32[512]{0:T(512)S(1)} %add_rsqrt_fusion, f32[16]{0:T(128)S(1)} %convert_divide_fusion, s32[16]{0:T(128)S(1)} %copy-done.4, s32[512]{0:T(512)S(1)} %get-tuple-element.12, ...), kind=kOutput, calls=%fused_computation.12 | convolution fusion | flops 4899610624 | bytes 11125888 | tf_op jit(solution)/shard_map/dot_general | solution.py:377
  58.5 0.0 copy-start
  58.5 0.4 fusion.14
  58.9 0.8 dynamic_slice.3
  59.7 0.1 copy-done
  59.8 32.3 %mix.1 = (f32[16,768]{1,0:T(8,128)S(1)}, bf16[4,2,4,16,768]{4,3,2,1,0:T(8,128)(2,1)S(1)}) custom-call(bf16[8,16,384]{2,1,0:T(8,128)(2,1)S(1)} %bitcast.42, bf16[4,16,384]{2,1,0:T(8,128)(2,1)S(1)} %bitcast.43, bf16[384,1536]{1,0:T(8,128)(2,1)S(1)} %copy-done, bf16[192,768]{1,0:T(8,128)(2,1)S(1)} %copy-done.1, f32[1,384]{1,0:T(1,128)S(1)} %broadcast_in_dim.2.gain_ref), custom_call_target="tpu_custom_call" | custom-call | tf_op jit(solution)/shard_map/mix/pallas_call | solution.py:290
  92.1 0.2 convert_reduce_fusion
  92.2 2.9 %multiply_reduce_fusion = (f32[]{:T(128)}, f32[768,768]{1,0:T(8,128)}) fusion(f32[768]{0:T(1024)S(1)} %broadcast_multiply_fusion, bf16[4,2,4,16,768]{4,3,2,1,0:T(8,128)(2,1)S(1)} %get-tuple-element.8), kind=kOutput, calls=%fused_computation.20 | convolution fusion | flops 608698368 | bytes 3148804 | tf_op jit(solution)/shard_map/dot_general | solution.py:389
  95.8 0.0 copy-start.3
  95.8 2.7 %fusion.29 = f32[16,768]{1,0:T(8,128)S(1)} fusion(f32[768,768]{1,0:T(8,128)} %get-tuple-element.10, f32[]{:T(128)S(6)} %div.55, f32[16,768]{1,0:T(8,128)S(1)} %get-tuple-element.7, f32[768]{0:T(1024)S(1)} %broadcast_multiply_fusion), kind=kOutput, calls=%fused_computation.33 | convolution fusion | flops 59019264 | bytes 2460676 | tf_op jit(solution)/shard_map/dot_general | solution.py:16
  98.4 0.0 copy-done.3
  98.5 3.2 %fusion.15 = f32[768,768]{1,0:T(8,128)S(1)} fusion(f32[768,768]{1,0:T(8,128)S(1)} %copy-done.3, f32[]{:T(128)S(6)} %div.55), kind=kOutput, calls=%fused_computation.24 | convolution fusion | flops 2720268288 | bytes 4718596 | tf_op jit(solution)/shard_map/dot_general | solution.py:16
  101.7 0.8 convolution_add_fusion.1
  102.4 3.1 %fusion.51 = f32[768,768]{1,0:T(8,128)S(1)} fusion(f32[768,768]{1,0:T(8,128)S(1)} %fusion.15), kind=kOutput, calls=%fused_computation.71 | convolution fusion | flops 2717908992 | bytes 4718592 | tf_op jit(solution)/shard_map/dot_general | solution.py:16
  105.6 0.8 convolution_add_fusion
  106.4 0.8 fusion.52
  107.1 0.8 fusion.31
  107.9 0.2 convert_reduce_fusion.1
  108.1 0.8 fusion.30.out_ref
  108.9 6.1 %route.1 = bf16[4,8,768]{2,1,0:T(8,128)(2,1)} custom-call(bf16[4,8,768]{2,1,0:T(8,128)(2,1)} %fusion.30.out_ref), custom_call_target="tpu_custom_call" | custom-call | tf_op jit(solution)/shard_map/route/pallas_call | solution.py:338
  114.9 1.4 %copy.21 = bf16[32,768]{1,0:T(8,128)(2,1)} copy(bf16[32,768]{1,0:T(8,128)(2,1)} %bitcast.45) | data formatting | bytes 98304
  (19 shorter events, 0.1 us)
Async XLA Ops:
  0.0 49.3 %copy-start.2 = (bf16[512,1536]{1,0:T(8,128)(2,1)S(1)}, bf16[512,1536]{1,0:T(8,128)(2,1)}, u32[]{:S(2)}) copy-start(bf16[512,1536]{1,0:T(8,128)(2,1)} %param.8) | copy-start | bytes 4718596
  0.0 49.7 %copy-start.5 = (f32[1536]{0:T(1024)S(1)}, f32[1536]{0:T(1024)}, u32[]{:S(2)}) copy-start(f32[1536]{0:T(1024)} %param.10) | copy-start | bytes 18436
  0.0 49.7 %copy-start.4 = (s32[16]{0:T(128)S(1)}, s32[16]{0:T(128)}, u32[]{:S(2)}) copy-start(s32[16]{0:T(128)} %param.9) | copy-start | bytes 196
  49.7 10.0 %copy-start.1 = (bf16[192,768]{1,0:T(8,128)(2,1)S(1)}, bf16[192,768]{1,0:T(8,128)(2,1)}, u32[]{:S(2)}) copy-start(bf16[192,768]{1,0:T(8,128)(2,1)} %proj_ref.1) | copy-start | bytes 884740
  58.5 1.3 %copy-start = (bf16[384,1536]{1,0:T(8,128)(2,1)S(1)}, bf16[384,1536]{1,0:T(8,128)(2,1)}, u32[]{:S(2)}) copy-start(bf16[384,1536]{1,0:T(8,128)(2,1)} %down_ref.1) | copy-start | bytes 3538948
  95.8 2.7 %copy-start.3 = (f32[768,768]{1,0:T(8,128)S(1)}, f32[768,768]{1,0:T(8,128)}, u32[]{:S(2)}) copy-start(f32[768,768]{1,0:T(8,128)} %get-tuple-element.10) | copy-start | bytes 7077892
  106.4 1.6 %copy-start.6 = (s32[16,1]{0,1:T(1,128)S(1)}, s32[16,1]{0,1:T(1,128)}, u32[]{:S(2)}) copy-start(s32[16,1]{0,1:T(1,128)} %param.15) | copy-start | bytes 196

commit v5 on v4

--- a/solution.py
+++ b/solution.py
@@ -131,11 +131,12 @@
 
     start_z(0)
     start_z(1)
-    own.start()
-    p_copies.append(send(up_ref, full_ref.at[row_at(z), :], p_send, p_recv, partner))
     for step in range(CHUNKS + 2):
         if step < CHUNKS:
             spread(step)
+        if step == 0:
+            own.start()
+            p_copies.append(send(up_ref, full_ref.at[row_at(z), :], p_send, p_recv, partner))
         if 0 <= step - 1 < CHUNKS:
             relay(step - 1)
         if step >= 2:
@@ -393,12 +394,14 @@
     magnitude = jnp.sqrt(jnp.sum(covariance * covariance))
     s1 = eye - (2.0 / magnitude) * covariance
     s2 = fdot(s1, s1)
-    s4 = fdot(s2, s2)
     rows = (embedded - average) * (2.0 / magnitude)
     rows = rows + fdot(rows, s1)
     rows = rows + fdot(rows, s2)
-    rows = rows + fdot(rows, s4)
-    rows = rows + fdot(fdot(rows, s4), s4)
+    rows = rows + fdot(fdot(rows, s2), s2)
+    eighth = rows
+    for _ in range(4):
+        eighth = fdot(eighth, s2)
+    rows = rows + eighth
     whitened = rows.astype(jnp.bfloat16)
     capacity = 2 * pass_rows // n_dp
     target_owner = owners[:, 0]

time: 117 us -> 123 us (1.051)
  Pallas kernels: 87.6 us -> 95 us
    pallas_call x1, Pallas kernels: 49.3 us -> 55.5 us  [gather_up(): pl.pallas_call(functools.partial(gather_kernel, nz), out_shape=jax.ShapeD...]
    dot_general x7 -> x9, matrix products: 12.1 us -> 11.3 us  [fdot(): return jnp.dot(a, b, precision=HIGH, preferred_element_type=jnp.float32)]
where the time goes in v5:
time: 123 us
  Pallas kernels  95 us (77%)
  matrix products  24 us (20%)
  local copies, waits for them, and re-layouts  2.32 us (2%)
    pallas_call x1, Pallas kernels, gather_up(): pl.pallas_call(functools.partial(gather_kernel, nz), out_shape=jax.ShapeD...  55.5 us
    pallas_call x1, Pallas kernels, mix(): pl.pallas_call(functools.partial(mix_kernel, n_dp, n_fsdp, float(width)),...  33.4 us
    dot_general x9, matrix products, fdot(): return jnp.dot(a, b, precision=HIGH, preferred_element_type=jnp.float32)  11.3 us
    dot_general x1, matrix products, on_device(): jnp.dot(inside, activated, preferred_element_type=jnp.float32) * inverse  8.73 us
    pallas_call x1, Pallas kernels, route(): pl.pallas_call(functools.partial(route_kernel, n_dp), out_shape=jax.Shape...  6.15 us
    dot_general x1, matrix products, on_device(): jnp.dot(everyone.T, everyone, preferred_element_type=jnp.float32)  2.86 us

profile of v5, /device:TPU:0, one launch (start us, length us, event | category | flops | bytes accessed | tf_op | source)
XLA Modules:
  0.0 122.9 jit_solution(13532069500141310415)
XLA Ops:
  0.0 55.5 %gather_up.1 = bf16[1536,3072]{1,0:T(8,128)(2,1)} custom-call(bf16[192,3072]{1,0:T(8,128)(2,1)} %up_ref.1), custom_call_target="tpu_custom_call" | custom-call | tf_op jit(solution)/shard_map/gather_up/pallas_call | solution.py:155
  55.5 0.4 fusion.9
  56.0 0.0 copy-start.1
  56.0 8.7 %fusion.8 = bf16[16,3072]{1,0:T(8,128)(2,1)S(1)} fusion(bf16[1536,3072]{1,0:T(8,128)(2,1)} %gather_up.1, bf16[512,1536]{1,0:T(8,128)(2,1)S(1)} %copy-done.2, f32[1536]{0:T(1024)S(1)} %copy-done.5, f32[512]{0:T(512)S(1)} %add_rsqrt_fusion, f32[16]{0:T(128)S(1)} %convert_divide_fusion, s32[16]{0:T(128)S(1)} %copy-done.4, s32[512]{0:T(512)S(1)} %get-tuple-element.12, ...), kind=kOutput, calls=%fused_computation.12 | convolution fusion | flops 4899610624 | bytes 11125888 | tf_op jit(solution)/shard_map/dot_general | solution.py:378
  64.7 0.0 copy-start
  64.8 0.4 fusion.14
  65.2 0.8 dynamic_slice.3
  65.9 0.1 copy-done
  66.0 33.4 %mix.1 = (f32[16,768]{1,0:T(8,128)S(1)}, bf16[4,2,4,16,768]{4,3,2,1,0:T(8,128)(2,1)S(1)}) custom-call(bf16[8,16,384]{2,1,0:T(8,128)(2,1)S(1)} %bitcast.46, bf16[4,16,384]{2,1,0:T(8,128)(2,1)S(1)} %bitcast.47, bf16[384,1536]{1,0:T(8,128)(2,1)S(1)} %copy-done, bf16[192,768]{1,0:T(8,128)(2,1)S(1)} %copy-done.1, f32[1,384]{1,0:T(1,128)S(1)} %broadcast_in_dim.2.gain_ref), custom_call_target="tpu_custom_call" | custom-call | tf_op jit(solution)/shard_map/mix/pallas_call | solution.py:291
  99.4 0.2 convert_reduce_fusion
  99.5 2.9 %multiply_reduce_fusion = (f32[]{:T(128)}, f32[768,768]{1,0:T(8,128)}) fusion(f32[768]{0:T(1024)S(1)} %broadcast_multiply_fusion, bf16[4,2,4,16,768]{4,3,2,1,0:T(8,128)(2,1)S(1)} %get-tuple-element.8), kind=kOutput, calls=%fused_computation.20 | convolution fusion | flops 608698368 | bytes 3148804 | tf_op jit(solution)/shard_map/dot_general | solution.py:390
  103.1 2.7 %fusion.29 = f32[16,768]{1,0:T(8,128)S(1)} fusion(f32[768,768]{1,0:T(8,128)} %get-tuple-element.10, f32[]{:T(128)S(6)} %div.55, f32[16,768]{1,0:T(8,128)S(1)} %get-tuple-element.7, f32[768]{0:T(1024)S(1)} %broadcast_multiply_fusion), kind=kOutput, calls=%fused_computation.33 | convolution fusion | flops 59019264 | bytes 2460676 | tf_op jit(solution)/shard_map/dot_general | solution.py:16
  105.8 3.2 %fusion.15 = f32[768,768]{1,0:T(8,128)S(1)} fusion(f32[768,768]{1,0:T(8,128)S(1)} %copy-done.3, f32[]{:T(128)S(6)} %div.55), kind=kOutput, calls=%fused_computation.24 | convolution fusion | flops 2720268288 | bytes 4718596 | tf_op jit(solution)/shard_map/dot_general | solution.py:16
  109.0 0.8 convolution_add_fusion
  109.7 0.8 fusion.51
  110.5 0.8 convolution_add_fusion.2
  111.3 0.8 fusion.52
  112.1 0.8 fusion.53
  112.8 0.8 fusion.54
  113.6 0.8 fusion.31
  114.4 0.2 convert_reduce_fusion.1
  114.6 0.8 fusion.30.out_ref
  115.3 6.1 %route.1 = bf16[4,8,768]{2,1,0:T(8,128)(2,1)} custom-call(bf16[4,8,768]{2,1,0:T(8,128)(2,1)} %fusion.30.out_ref), custom_call_target="tpu_custom_call" | custom-call | tf_op jit(solution)/shard_map/route/pallas_call | solution.py:339
  121.5 1.4 %copy.21 = bf16[32,768]{1,0:T(8,128)(2,1)} copy(bf16[32,768]{1,0:T(8,128)(2,1)} %bitcast.49) | data formatting | bytes 98304
  (21 shorter events, 0.1 us)
Async XLA Ops:
  0.0 55.5 %copy-start.2 = (bf16[512,1536]{1,0:T(8,128)(2,1)S(1)}, bf16[512,1536]{1,0:T(8,128)(2,1)}, u32[]{:S(2)}) copy-start(bf16[512,1536]{1,0:T(8,128)(2,1)} %param.8) | copy-start | bytes 4718596
  0.0 56.0 %copy-start.5 = (f32[1536]{0:T(1024)S(1)}, f32[1536]{0:T(1024)}, u32[]{:S(2)}) copy-start(f32[1536]{0:T(1024)} %param.10) | copy-start | bytes 18436
  0.0 55.9 %copy-start.4 = (s32[16]{0:T(128)S(1)}, s32[16]{0:T(128)}, u32[]{:S(2)}) copy-start(s32[16]{0:T(128)} %param.9) | copy-start | bytes 196
  56.0 10.0 %copy-start.1 = (bf16[192,768]{1,0:T(8,128)(2,1)S(1)}, bf16[192,768]{1,0:T(8,128)(2,1)}, u32[]{:S(2)}) copy-start(bf16[192,768]{1,0:T(8,128)(2,1)} %proj_ref.1) | copy-start | bytes 884740
  64.7 1.3 %copy-start = (bf16[384,1536]{1,0:T(8,128)(2,1)S(1)}, bf16[384,1536]{1,0:T(8,128)(2,1)}, u32[]{:S(2)}) copy-start(bf16[384,1536]{1,0:T(8,128)(2,1)} %down_ref.1) | copy-start | bytes 3538948
  103.1 2.7 %copy-start.3 = (f32[768,768]{1,0:T(8,128)S(1)}, f32[768,768]{1,0:T(8,128)}, u32[]{:S(2)}) copy-start(f32[768,768]{1,0:T(8,128)} %get-tuple-element.10) | copy-start | bytes 7077892
  112.8 1.6 %copy-start.6 = (s32[16,1]{0,1:T(1,128)S(1)}, s32[16,1]{0,1:T(1,128)}, u32[]{:S(2)}) copy-start(s32[16,1]{0,1:T(1,128)} %param.15) | copy-start | bytes 196
